TPU v7x, 128 devices: a whole 4x4x4 slice. The times are simulated.
128 devices in a mesh: curve: 128 (over y, x, z, core).
Axes of the slice: x: 4, y: 4, z: 4, core: 2. Of those that a mesh axis runs over, the one named last changes fastest.
Arguments:
- diag_blocks: bfloat16 [8192, 128, 128], P('curve'), may hold values from 0.049804688 to 1
- super_blocks: bfloat16 [8192, 4, 128, 128], P('curve'), may hold values from 0.049804688 to 1
- far_blocks: bfloat16 [32768, 128, 128], P('curve'), may hold values from 0.049804688 to 1
- far_row: int32 [32768], P('curve'), may hold values from -1 to 63, as said below
- send_slot: int32 [32768], P('curve'), may hold values from -1 to 63, as said below
- start_panel: float32 [64, 1048576], P(None, 'curve'), may hold values from -6 to 6
Outputs:
- basis: float32 [64, 1048576], P(None, 'curve')
- update: float32 [64, 1048576], P(None, 'curve')
Inputs may be any that keep to these rules, and one draw needn't show every extreme that they name: `send_slot`: at most 2 live slots from one owner to one reader; some owner fills all 2 slots to every reader. `far_row`: empty slots match those of send_slot.
All inputs are finite; a program needn't handle non-finite values.
Results may differ from a plain program's by a relative error of at most 0.0026.
Values may be sent and summed in bfloat16 or wider, within the bound.
A program may use at most 256 MiB of HBM per device.

v0:
```python
import jax
import jax.numpy as jnp
from jax import lax
from jax.sharding import PartitionSpec as P

ITERS = 2


exact_mode = lax.Precision.HIGHEST
step_size = 10.0
momentum = 0.5


def extended_2(array, sides, width):
    for axis, dim in sides:
        size, length = (lax.axis_size(axis), array.shape[dim])
        up = [(i, (i + 1) % size) for i in range(size)]
        down = [(j, i) for i, j in up]
        last = lax.slice_in_dim(array, length - width, length, axis=dim)
        initial = lax.slice_in_dim(array, 0, width, axis=dim)
        before = lax.ppermute(last, axis, up)
        after = lax.ppermute(initial, axis, down)
        array = jnp.concatenate([before, array, after], axis=dim)
    return array


def passed_along(block, axis, distance):
    devices = range(lax.axis_size(axis))
    route = [((i - distance) % len(devices), i) for i in devices]
    return lax.ppermute(block, axis, route)


def gram_of(first, second):
    return jnp.einsum("bip,bjp->ij", first, second, precision=exact_mode)


def lower_inverse(cross):
    factor = jnp.linalg.cholesky(cross)
    return lax.linalg.triangular_solve(
        factor, jnp.eye(cross.shape[0], dtype=cross.dtype), left_side=True, lower=True
    )


def left_apply(matrix, blocks):
    return jnp.einsum("ij,bjp->bip", matrix, blocks, precision=exact_mode)


def near_apply(panel, diag_blocks, super_blocks, edge_supers):
    bands = super_blocks.shape[1]
    rows_dev = panel.shape[0]
    extended = extended_2(panel, (("curve", 0),), bands)
    supers_ext = jnp.concatenate([edge_supers, super_blocks], axis=0)
    result = jnp.einsum("bcp,bqp->bcq", panel, diag_blocks, preferred_element_type=jnp.float32)
    result = result + jnp.einsum(
        "bcp,bpq->bcq", panel, diag_blocks, preferred_element_type=jnp.float32
    )
    for band in range(bands):
        ahead = extended[bands + band + 1 : bands + band + 1 + rows_dev]
        result = result + jnp.einsum(
            "bcp,bqp->bcq", ahead, super_blocks[:, band], preferred_element_type=jnp.float32
        )
        first = bands - band - 1
        behind = extended[first : first + rows_dev]
        result = result + jnp.einsum(
            "bcp,bpq->bcq",
            behind,
            supers_ext[first : first + rows_dev, band],
            preferred_element_type=jnp.float32,
        )
    return result


def shards(diag_blocks, super_blocks, far_blocks, far_row, send_slot, start_panel):
    bands = super_blocks.shape[1]
    rows_dev = diag_blocks.shape[0]
    block_size = diag_blocks.shape[1]
    width = start_panel.shape[0]
    total_points = rows_dev * block_size * lax.axis_size("curve")
    edge_supers = passed_along(super_blocks[rows_dev - bands :], "curve", 1)
    send_live = (send_slot >= 0)[:, None, None]
    send_index = jnp.maximum(send_slot, 0)
    recv_live = (far_row >= 0)[:, None, None]
    recv_index = jnp.maximum(far_row, 0)

    def apply_w(panel):
        result = near_apply(panel, diag_blocks, super_blocks, edge_supers)
        outgoing = jnp.where(send_live, panel[send_index], jnp.zeros((), jnp.bfloat16))
        incoming = lax.all_to_all(outgoing, "curve", split_axis=0, concat_axis=0, tiled=True)
        forward = jnp.einsum(
            "fcp,fqp->fcq", incoming, far_blocks, preferred_element_type=jnp.float32
        )
        result = result.at[recv_index].add(jnp.where(recv_live, forward, 0.0))
        mirror = jnp.einsum(
            "fcp,fpq->fcq", panel[recv_index], far_blocks, preferred_element_type=jnp.float32
        )
        mirror = jnp.where(recv_live, mirror, 0.0)
        returned = lax.all_to_all(mirror, "curve", split_axis=0, concat_axis=0, tiled=True)
        result = result.at[send_index].add(jnp.where(send_live, returned, 0.0))
        return result

    unit_panel = jnp.ones((rows_dev, 1, block_size), jnp.bfloat16)
    inv_root = lax.rsqrt(apply_w(unit_panel))
    start_blocks = start_panel.reshape(width, rows_dev, block_size).transpose(1, 0, 2)
    start_gram = lax.psum(gram_of(start_blocks, start_blocks), "curve") / total_points
    current = left_apply(lower_inverse(start_gram), start_blocks)
    change = jnp.zeros_like(current)
    for step in range(ITERS):
        scaled = (inv_root * current).astype(jnp.bfloat16)
        image = inv_root * apply_w(scaled)
        rayleigh = lax.psum(gram_of(current, image), "curve") / total_points
        resid = image - left_apply(rayleigh.T, current)
        trial = current + step_size * resid + momentum * change
        cross = lax.psum(gram_of(trial, trial), "curve") / total_points
        fresh = left_apply(lower_inverse(cross), trial)
        change = fresh - current
        current = fresh
    basis = current.transpose(1, 0, 2).reshape(width, rows_dev * block_size)
    update = change.transpose(1, 0, 2).reshape(width, rows_dev * block_size)
    return (basis, update)


def solution(mesh):
    return jax.shard_map(
        shards,
        mesh=mesh,
        in_specs=(
            P("curve", None, None),
            P("curve", None, None, None),
            P("curve", None, None),
            P("curve"),
            P("curve"),
            P(None, "curve"),
        ),
        out_specs=(P(None, "curve"), P(None, "curve")),
        check_vma=False,
    )
```

profile of v0, /device:TPU:1, one launch (start us, length us, event | category | flops | bytes accessed | tf_op | source)
XLA Modules:
  0.0 953.1 jit_solution(4395993751826965920)
XLA Ops:
  7.6 10.2 %all-to-all-start = ((bf16[128,2,128]{2,1,0:T(2,128)(2,1)}), bf16[128,2,128]{2,1,0:T(2,128)(2,1)S(1)}, u32[]{:S(2)}, u32[]{:S(2)}) async-start(bf16[128,2,128]{2,1,0:T(2,128)(2,1)} %bitcast.265), calls=%async_computation | async-start | bytes 131072 | tf_op jit(solution)/shard_map/all_to_all | solution.py:88
  17.8 10.4 %copy.58 = bf16[64,4,128,128]{3,2,0,1:T(8,128)(2,1)} copy(bf16[64,4,128,128]{3,2,1,0:T(8,128)(2,1)} %param.10) | data formatting | bytes 16777216 | tf_op args[1]
  36.0 66.3 %psum.35 = f32[64,64]{0,1:T(8,128)S(1)} all-reduce(f32[64,64]{0,1:T(8,128)S(1)} %fusion.51), channel_id=1, replica_groups=mesh['curve'=128] {'curve'}, use_global_device_ids=true, to_apply=%region_0.1 | all-reduce | flops 4096 | bytes 32768 | tf_op jit(solution)/shard_map/psum | solution.py:104
  102.4 5.8 cholesky.59
  137.4 6.0 all-to-all-start.1
  144.3 7.8 fusion.66
  153.0 10.5 %constant_dynamic-update-slice_fusion = bf16[68,4,128,128]{3,2,0,1:T(8,128)(2,1)} fusion(bf16[68,4,128,128]{3,2,0,1:T(8,128)(2,1)} %constant_dynamic-update-slice_fusion.1, bf16[64,4,128,128]{3,2,1,0:T(8,128)(2,1)} %param.10), kind=kLoop, calls=%fused_computation.180 | loop fusion | bytes 16777216 | tf_op jit(solution)/shard_map/concatenate | solution.py:52
  196.8 11.0 %all-to-all-start.2 = ((bf16[256,64,128]{2,1,0:T(8,128)(2,1)}), bf16[256,64,128]{2,1,0:T(8,128)(2,1)}, u32[]{:S(2)}, u32[]{:S(2)}) async-start(bf16[256,64,128]{2,1,0:T(8,128)(2,1)} %broadcast_select_fusion.7), calls=%async_computation.2 | async-start | bytes 8388608 | tf_op jit(solution)/shard_map/all_to_all | solution.py:88
  207.9 10.3 %broadcast_select_fusion.4 = f32[256,64,128]{2,1,0:T(8,128)} fusion(pred[256]{0:T(512)(128)(4,1)S(1)} %broadcast_compare_fusion.1, bf16[256,64,128]{2,1,0:T(8,128)(2,1)} %gather_fusion.3, bf16[256,128,128]{2,1,0:T(8,128)(2,1)} %param.11), kind=kOutput, calls=%fused_computation.16 | convolution fusion | flops 538968064 | bytes 20971776 | tf_op jit(solution)/shard_map/fcp,fpq->fcq/dot_general | solution.py:93
  233.9 26.7 %all-to-all-done.2 = bf16[256,64,128]{2,1,0:T(8,128)(2,1)} async-done(((bf16[256,64,128]{2,1,0:T(8,128)(2,1)}), bf16[256,64,128]{2,1,0:T(8,128)(2,1)}, u32[]{:S(2)}, u32[]{:S(2)}) %all-to-all-start.2) | async-done | bytes 4194336 | tf_op jit(solution)/shard_map/all_to_all | solution.py:88
  260.6 6.3 all-to-all-start.3
  280.3 6.1 add_add_fusion.1
  286.5 11.3 %broadcast_select_fusion.5 = f32[256,64,128]{2,1,0:T(8,128)} fusion(pred[256]{0:T(512)(128)(4,1)S(1)} %copy-done.18, bf16[256,64,128]{2,1,0:T(8,128)(2,1)} %all-to-all-done.2, bf16[256,128,128]{2,1,0:T(8,128)(2,1)S(1)} %bitcast.267), kind=kOutput, calls=%fused_computation.17 | convolution fusion | flops 538968064 | bytes 20971776 | tf_op jit(solution)/shard_map/fcp,fqp->fcq/dot_general | solution.py:89
  297.8 39.0 %scatter_fusion = f32[64,64,128]{2,1,0:T(8,128)} fusion(f32[64,64,128]{2,1,0:T(8,128)} %add_add_fusion.1, s32[256]{0:T(256)S(1)} %copy-done.31, f32[256,64,128]{2,1,0:T(8,128)} %broadcast_select_fusion.5), kind=kCustom, calls=%fused_computation.8 | custom fusion | flops 2097152 | bytes 25166848 | tf_op jit(solution)/shard_map/scatter-add | solution.py:92
  336.8 31.5 %all-to-all-done.3 = f32[256,64,128]{2,1,0:T(8,128)} async-done(((f32[256,64,128]{2,1,0:T(8,128)}), f32[256,64,128]{2,1,0:T(8,128)}, u32[]{:S(2)}, u32[]{:S(2)}) %all-to-all-start.3) | async-done | bytes 8388640 | tf_op jit(solution)/shard_map/all_to_all | solution.py:97
  368.3 6.0 broadcast_select_fusion.3
  374.3 39.2 %scatter_fusion.1 = f32[64,64,128]{2,1,0:T(8,128)} fusion(f32[64,64,128]{2,1,0:T(8,128)} %scatter_fusion, s32[256]{0:T(256)S(1)} %copy-done.28, f32[256,64,128]{2,1,0:T(8,128)} %broadcast_select_fusion.3), kind=kCustom, calls=%fused_computation.9 | custom fusion | flops 2097152 | bytes 25166848 | tf_op jit(solution)/shard_map/scatter-add | solution.py:98
  417.7 66.9 %psum.36 = f32[64,64]{0,1:T(8,128)S(1)} all-reduce(f32[64,64]{0,1:T(8,128)S(1)} %fusion.52), channel_id=1, replica_groups=mesh['curve'=128] {'curve'}, use_global_device_ids=true, to_apply=%region_7.10 | all-reduce | flops 4096 | bytes 32768 | tf_op jit(solution)/shard_map/psum | solution.py:110
  492.8 63.1 %psum.37 = f32[64,64]{0,1:T(8,128)S(1)} all-reduce(f32[64,64]{0,1:T(8,128)S(1)} %convolution_bitcast_fusion.3), channel_id=1, replica_groups=mesh['curve'=128] {'curve'}, use_global_device_ids=true, to_apply=%region_8.11 | all-reduce | flops 4096 | bytes 32768 | tf_op jit(solution)/shard_map/psum | solution.py:113
  556.0 5.8 cholesky.70
  587.4 11.6 %all-to-all-start.4 = ((bf16[256,64,128]{2,1,0:T(8,128)(2,1)}), bf16[256,64,128]{2,1,0:T(8,128)(2,1)}, u32[]{:S(2)}, u32[]{:S(2)}) async-start(bf16[256,64,128]{2,1,0:T(8,128)(2,1)} %broadcast_select_fusion.6), calls=%async_computation.4 | async-start | bytes 8388608 | tf_op jit(solution)/shard_map/all_to_all | solution.py:88
  599.1 10.3 %broadcast_select_fusion.1 = f32[256,64,128]{2,1,0:T(8,128)} fusion(pred[256]{0:T(512)(128)(4,1)S(1)} %copy-done.18, bf16[256,64,128]{2,1,0:T(8,128)(2,1)} %gather_fusion.5, bf16[256,128,128]{2,1,0:T(8,128)(2,1)} %param.11), kind=kOutput, calls=%fused_computation.13 | convolution fusion | flops 538968064 | bytes 20971776 | tf_op jit(solution)/shard_map/fcp,fpq->fcq/dot_general | solution.py:93
  625.1 26.8 %all-to-all-done.4 = bf16[256,64,128]{2,1,0:T(8,128)(2,1)} async-done(((bf16[256,64,128]{2,1,0:T(8,128)(2,1)}), bf16[256,64,128]{2,1,0:T(8,128)(2,1)}, u32[]{:S(2)}, u32[]{:S(2)}) %all-to-all-start.4) | async-done | bytes 4194336 | tf_op jit(solution)/shard_map/all_to_all | solution.py:88
  651.8 6.3 all-to-all-start.5
  676.4 11.3 %broadcast_select_fusion.2 = f32[256,64,128]{2,1,0:T(8,128)} fusion(pred[256]{0:T(512)(128)(4,1)S(1)} %copy-done.19, bf16[256,64,128]{2,1,0:T(8,128)(2,1)} %all-to-all-done.4, bf16[256,128,128]{2,1,0:T(8,128)(2,1)S(1)} %bitcast.269), kind=kOutput, calls=%fused_computation.14 | convolution fusion | flops 538968064 | bytes 20971776 | tf_op jit(solution)/shard_map/fcp,fqp->fcq/dot_general | solution.py:89
  687.8 26.2 %scatter_fusion.2 = f32[64,64,128]{2,1,0:T(8,128)S(1)} fusion(f32[64,64,128]{2,1,0:T(8,128)S(1)} %add_add_fusion, s32[256]{0:T(256)S(1)} %copy-done.32, f32[256,64,128]{2,1,0:T(8,128)} %broadcast_select_fusion.2), kind=kCustom, calls=%fused_computation.10 | custom fusion | flops 2097152 | bytes 25166848 | tf_op jit(solution)/shard_map/scatter-add | solution.py:92
  714.0 45.4 %all-to-all-done.5 = f32[256,64,128]{2,1,0:T(8,128)} async-done(((f32[256,64,128]{2,1,0:T(8,128)}), f32[256,64,128]{2,1,0:T(8,128)}, u32[]{:S(2)}, u32[]{:S(2)}) %all-to-all-start.5) | async-done | bytes 8388640 | tf_op jit(solution)/shard_map/all_to_all | solution.py:97
  759.4 6.0 broadcast_select_fusion
  765.5 26.3 %scatter_fusion.3 = f32[64,64,128]{2,1,0:T(8,128)S(1)} fusion(f32[64,64,128]{2,1,0:T(8,128)S(1)} %scatter_fusion.2, s32[256]{0:T(256)S(1)} %copy-done.29, f32[256,64,128]{2,1,0:T(8,128)} %broadcast_select_fusion), kind=kCustom, calls=%fused_computation.11 | custom fusion | flops 2097152 | bytes 25166848 | tf_op jit(solution)/shard_map/scatter-add | solution.py:98
  795.3 66.9 %psum.38 = f32[64,64]{0,1:T(8,128)S(1)} all-reduce(f32[64,64]{0,1:T(8,128)S(1)} %fusion.57), channel_id=1, replica_groups=mesh['curve'=128] {'curve'}, use_global_device_ids=true, to_apply=%region_11.14 | all-reduce | flops 4096 | bytes 32768 | tf_op jit(solution)/shard_map/psum | solution.py:110
  870.7 63.1 %psum.39 = f32[64,64]{0,1:T(8,128)S(1)} all-reduce(f32[64,64]{0,1:T(8,128)S(1)} %convolution_bitcast_fusion.1), channel_id=1, replica_groups=mesh['curve'=128] {'curve'}, use_global_device_ids=true, to_apply=%region_12.15 | all-reduce | flops 4096 | bytes 32768 | tf_op jit(solution)/shard_map/psum | solution.py:113
  933.9 5.8 cholesky.81
  (228 shorter events, 205.2 us)
Async XLA Ops:
  0.6 30.5 %copy-start = (bf16[64,128,128]{2,1,0:T(8,128)(2,1)S(1)}, bf16[64,128,128]{2,1,0:T(8,128)(2,1)}, u32[]{:S(2)}) copy-start(bf16[64,128,128]{2,1,0:T(8,128)(2,1)} %param.9) | copy-start | bytes 6291460
  0.7 135.5 %collective-permute-start.1 = (bf16[4,1,128]{2,0,1:T(4,128)(2,1)S(1)}, bf16[4,1,128]{2,0,1:T(4,128)(2,1)S(1)}, u32[]{:S(2)}, u32[]{:S(2)}) collective-permute-start(bf16[4,1,128]{2,0,1:T(4,128)(2,1)S(1)} %broadcast.92), channel_id=1, source_target_pairs={{0,1},{1,2},{2,3},{3,4},{4,5},{5,6},{6,7},{7,8},{8,9},{9,10},{10,1... | collective-permute-start | bytes 3080 | tf_op jit(solution)/shard_map/ppermute | solution.py:21
  3.8 118.8 %collective-permute-start = (bf16[4,1,128]{2,0,1:T(4,128)(2,1)S(1)}, bf16[4,1,128]{2,0,1:T(4,128)(2,1)S(1)}, u32[]{:S(2)}, u32[]{:S(2)}) collective-permute-start(bf16[4,1,128]{2,0,1:T(4,128)(2,1)S(1)} %broadcast.92), channel_id=1, source_target_pairs={{1,0},{2,1},{3,2},{4,3},{5,4},{6,5},{7,6},{8,7},{9,8},{10,9},{11,1... | collective-permute-start | bytes 3080 | tf_op jit(solution)/shard_map/ppermute | solution.py:22
  4.4 188.4 %copy-start.24 = (pred[256]{0:T(512)(128)(4,1)}, pred[256]{0:T(512)(128)(4,1)S(1)}, u32[]{:S(2)}) copy-start(pred[256]{0:T(512)(128)(4,1)S(1)} %broadcast_compare_fusion) | copy-start | bytes 772
  5.1 169.7 %copy-start.27 = (s32[256]{0:T(256)}, s32[256]{0:T(256)S(1)}, u32[]{:S(2)}) copy-start(s32[256]{0:T(256)S(1)} %broadcast_maximum_fusion) | copy-start | bytes 3076
  5.8 166.9 %copy-start.30 = (s32[256]{0:T(256)}, s32[256]{0:T(256)S(1)}, u32[]{:S(2)}) copy-start(s32[256]{0:T(256)S(1)} %broadcast_maximum_fusion.1) | copy-start | bytes 3076
  5.8 108.6 %copy-start.38 = (s32[1024]{0:T(1024)}, s32[1024]{0:T(1024)S(1)}, u32[]{:S(2)}) copy-start(s32[1024]{0:T(1024)S(1)} %get-tuple-element.20) | copy-start | bytes 12292
  7.6 129.2 %all-to-all-start = ((bf16[128,2,128]{2,1,0:T(2,128)(2,1)}), bf16[128,2,128]{2,1,0:T(2,128)(2,1)S(1)}, u32[]{:S(2)}, u32[]{:S(2)}) async-start(bf16[128,2,128]{2,1,0:T(2,128)(2,1)} %bitcast.265), calls=%async_computation | async-start | bytes 131072 | tf_op jit(solution)/shard_map/all_to_all | solution.py:88
  17.8 13.3 %copy-start.39 = (s32[256]{0:T(256)S(1)}, s32[256]{0:T(256)}, u32[]{:S(2)}) copy-start(s32[256]{0:T(256)} %param.12) | copy-start | bytes 3076
  29.3 122.8 %collective-permute-start.2 = (bf16[4,4,128,128]{3,2,0,1:T(8,128)(2,1)S(1)}, bf16[4,4,128,128]{3,2,0,1:T(8,128)(2,1)S(1)}, u32[]{:S(2)}, u32[]{:S(2)}) collective-permute-start(bf16[4,4,128,128]{3,2,0,1:T(8,128)(2,1)S(1)} %slice.207), channel_id=1, source_target_pairs={{127,0},{0,1},{1,2},{2,3},{3,4},{4,5},{5,6},{6,7},{7,8},{8,9},{9,1... | collective-permute-start | bytes 1572872 | tf_op jit(solution)/shard_map/ppermute | solution.py:30
  31.1 176.7 %copy-start.17 = (pred[256]{0:T(512)(128)(4,1)}, pred[256]{0:T(512)(128)(4,1)S(1)}, u32[]{:S(2)}) copy-start(pred[256]{0:T(512)(128)(4,1)S(1)} %broadcast_compare_fusion.1) | copy-start | bytes 772
  137.4 37.4 %all-to-all-start.1 = ((f32[256,1,128]{2,1,0:T(1,128)}), f32[256,1,128]{2,1,0:T(1,128)S(1)}, u32[]{:S(2)}, u32[]{:S(2)}) async-start(f32[256,1,128]{2,1,0:T(1,128)} %bitcast.58), calls=%async_computation.1 | async-start | bytes 262144 | tf_op jit(solution)/shard_map/all_to_all | solution.py:97
  190.9 76.0 %collective-permute-start.4 = (bf16[4,64,128]{2,1,0:T(8,128)(2,1)}, bf16[4,64,128]{2,1,0:T(8,128)(2,1)}, u32[]{:S(2)}, u32[]{:S(2)}) collective-permute-start(bf16[4,64,128]{2,1,0:T(8,128)(2,1)} %get-tuple-element.6), channel_id=1, source_target_pairs={{0,1},{1,2},{2,3},{3,4},{4,5},{5,6},{6,7},{7,8},{8,9},{9,10},{10,1... | collective-permute-start | bytes 196616 | tf_op jit(solution)/shard_map/ppermute | solution.py:21
  192.9 28.2 %collective-permute-start.3 = (bf16[4,64,128]{2,1,0:T(8,128)(2,1)S(1)}, bf16[4,64,128]{2,1,0:T(8,128)(2,1)S(1)}, u32[]{:S(2)}, u32[]{:S(2)}) collective-permute-start(bf16[4,64,128]{2,1,0:T(8,128)(2,1)S(1)} %get-tuple-element.7), channel_id=1, source_target_pairs={{1,0},{2,1},{3,2},{4,3},{5,4},{6,5},{7,6},{8,7},{9,8},{10,9},{11,1... | collective-permute-start | bytes 196616 | tf_op jit(solution)/shard_map/ppermute | solution.py:22
  196.8 63.8 %all-to-all-start.2 = ((bf16[256,64,128]{2,1,0:T(8,128)(2,1)}), bf16[256,64,128]{2,1,0:T(8,128)(2,1)}, u32[]{:S(2)}, u32[]{:S(2)}) async-start(bf16[256,64,128]{2,1,0:T(8,128)(2,1)} %broadcast_select_fusion.7), calls=%async_computation.2 | async-start | bytes 8388608 | tf_op jit(solution)/shard_map/all_to_all | solution.py:88
  260.6 107.6 %all-to-all-start.3 = ((f32[256,64,128]{2,1,0:T(8,128)}), f32[256,64,128]{2,1,0:T(8,128)}, u32[]{:S(2)}, u32[]{:S(2)}) async-start(f32[256,64,128]{2,1,0:T(8,128)} %broadcast_select_fusion.4), calls=%async_computation.3 | async-start | bytes 16777216 | tf_op jit(solution)/shard_map/all_to_all | solution.py:97
  270.5 16.0 %slice-start = ((s8[8388608]{0:T(1024)(128)(4,1)}), s8[4194304]{0:T(1024)(128)(4,1)S(1)}, s32[]{:S(2)}) async-start(s8[8388608]{0:T(1024)(128)(4,1)} %bitcast.266), calls=%async_computation.6 | async-start | bytes 8388608
  274.3 12.2 %slice-start.1 = ((s8[8388608]{0:T(1024)(128)(4,1)}), s8[4194304]{0:T(1024)(128)(4,1)S(1)}, s32[]{:S(2)}) async-start(s8[8388608]{0:T(1024)(128)(4,1)} %bitcast.266), calls=%async_computation.7 | async-start | bytes 8388608
  286.5 11.3 %copy-start.31 = (s32[256]{0:T(256)S(1)}, s32[256]{0:T(256)}, u32[]{:S(2)}) copy-start(s32[256]{0:T(256)} %copy-done.30) | copy-start | bytes 3076
  297.8 70.5 %copy-start.25 = (pred[256]{0:T(512)(128)(4,1)S(1)}, pred[256]{0:T(512)(128)(4,1)}, u32[]{:S(2)}) copy-start(pred[256]{0:T(512)(128)(4,1)} %copy-done.24) | copy-start | bytes 772
  336.8 37.5 %copy-start.28 = (s32[256]{0:T(256)S(1)}, s32[256]{0:T(256)}, u32[]{:S(2)}) copy-start(s32[256]{0:T(256)} %copy-done.27) | copy-start | bytes 3076
  374.3 39.2 %copy-start.11 = (f32[64,128]{1,0:T(8,128)S(1)}, f32[64,128]{1,0:T(8,128)}, u32[]{:S(2)}) copy-start(f32[64,128]{1,0:T(8,128)} %copy-done.10) | copy-start | bytes 98308
  582.4 75.7 %collective-permute-start.6 = (bf16[4,64,128]{2,1,0:T(8,128)(2,1)}, bf16[4,64,128]{2,1,0:T(8,128)(2,1)}, u32[]{:S(2)}, u32[]{:S(2)}) collective-permute-start(bf16[4,64,128]{2,1,0:T(8,128)(2,1)} %get-tuple-element.4), channel_id=1, source_target_pairs={{0,1},{1,2},{2,3},{3,4},{4,5},{5,6},{6,7},{7,8},{8,9},{9,10},{10,1... | collective-permute-start | bytes 196616 | tf_op jit(solution)/shard_map/ppermute | solution.py:21
  583.2 29.0 %collective-permute-start.5 = (bf16[4,64,128]{2,1,0:T(8,128)(2,1)S(1)}, bf16[4,64,128]{2,1,0:T(8,128)(2,1)S(1)}, u32[]{:S(2)}, u32[]{:S(2)}) collective-permute-start(bf16[4,64,128]{2,1,0:T(8,128)(2,1)S(1)} %get-tuple-element.5), channel_id=1, source_target_pairs={{1,0},{2,1},{3,2},{4,3},{5,4},{6,5},{7,6},{8,7},{9,8},{10,9},{11,1... | collective-permute-start | bytes 196616 | tf_op jit(solution)/shard_map/ppermute | solution.py:22
  587.4 64.4 %all-to-all-start.4 = ((bf16[256,64,128]{2,1,0:T(8,128)(2,1)}), bf16[256,64,128]{2,1,0:T(8,128)(2,1)}, u32[]{:S(2)}, u32[]{:S(2)}) async-start(bf16[256,64,128]{2,1,0:T(8,128)(2,1)} %broadcast_select_fusion.6), calls=%async_computation.4 | async-start | bytes 8388608 | tf_op jit(solution)/shard_map/all_to_all | solution.py:88
  651.8 107.6 %all-to-all-start.5 = ((f32[256,64,128]{2,1,0:T(8,128)}), f32[256,64,128]{2,1,0:T(8,128)}, u32[]{:S(2)}, u32[]{:S(2)}) async-start(f32[256,64,128]{2,1,0:T(8,128)} %broadcast_select_fusion.1), calls=%async_computation.5 | async-start | bytes 16777216 | tf_op jit(solution)/shard_map/all_to_all | solution.py:97
  661.7 14.7 %slice-start.2 = ((s8[8388608]{0:T(1024)(128)(4,1)}), s8[4194304]{0:T(1024)(128)(4,1)S(1)}, s32[]{:S(2)}) async-start(s8[8388608]{0:T(1024)(128)(4,1)} %bitcast.268), calls=%async_computation.8 | async-start | bytes 8388608
  665.5 10.9 %slice-start.3 = ((s8[8388608]{0:T(1024)(128)(4,1)}), s8[4194304]{0:T(1024)(128)(4,1)S(1)}, s32[]{:S(2)}) async-start(s8[8388608]{0:T(1024)(128)(4,1)} %bitcast.268), calls=%async_computation.9 | async-start | bytes 8388608
  676.4 11.3 %copy-start.32 = (s32[256]{0:T(256)S(1)}, s32[256]{0:T(256)}, u32[]{:S(2)}) copy-start(s32[256]{0:T(256)} %copy-done.30) | copy-start | bytes 3076
  687.8 71.7 %copy-start.26 = (pred[256]{0:T(512)(128)(4,1)S(1)}, pred[256]{0:T(512)(128)(4,1)}, u32[]{:S(2)}) copy-start(pred[256]{0:T(512)(128)(4,1)} %copy-done.24) | copy-start | bytes 772
  714.0 51.5 %copy-start.29 = (s32[256]{0:T(256)S(1)}, s32[256]{0:T(256)}, u32[]{:S(2)}) copy-start(s32[256]{0:T(256)} %copy-done.27) | copy-start | bytes 3076
  765.5 26.3 %copy-start.12 = (f32[64,128]{1,0:T(8,128)S(1)}, f32[64,128]{1,0:T(8,128)}, u32[]{:S(2)}) copy-start(f32[64,128]{1,0:T(8,128)} %copy-done.10) | copy-start | bytes 98308
  (37 other events, 168.4 us)
where the time goes:
time: 962 us; the launch traced here: 953 us
  blocking collectives  326 us (34%)
  other arithmetic  196 us (20%)
  matrix products  189 us (20%)
  waiting for transfers between devices  130 us (14%)
  starting transfers between devices  59.2 us (6%)
  local copies, waits for them, and re-layouts  50.7 us (5%)
    psum x2, blocking collectives, shards(): rayleigh = lax.psum(gram_of(current, image), 'curve') / total_points  134 us
    psum x2, blocking collectives, shards(): cross = lax.psum(gram_of(trial, trial), 'curve') / total_points  126 us
    all_to_all x3, waiting for transfers between devices, apply_w(): lax.all_to_all(mirror, 'curve', split_axis=0, concat_axis=0, tiled=True)  76.9 us
    scatter-add x3, other arithmetic, apply_w(): result = result.at[send_index].add(jnp.where(send_live, returned, 0.0))  67.6 us
    scatter-add x3, other arithmetic, apply_w(): result = result.at[recv_index].add(jnp.where(recv_live, forward, 0.0))  67.3 us
    psum x1, blocking collectives, shards(): lax.psum(gram_of(start_blocks, start_blocks), 'curve') / total_points  66.3 us
    all_to_all x3, waiting for transfers between devices, apply_w(): lax.all_to_all(outgoing, 'curve', split_axis=0, concat_axis=0, tiled=True)  53.5 us
    dot_general x12, matrix products, near_apply(): jnp.einsum('bcp,bpq->bcq', behind, supers_ext[first:first + rows_dev, ban...  42.3 us
  transfers between devices with their start and end apart: 13, of which 4 were waited for; matrix products, arithmetic and copies ran while one was open for 28% of the time, Pallas kernels for 0%

commit v1 on v0

v1 whole, which is shorter than its diff:
```python
import functools

import jax
import jax.numpy as jnp
from jax import lax
from jax.experimental import pallas as pl
from jax.experimental.pallas import tpu as pltpu
from jax.sharding import PartitionSpec as P

f32, bf16, i32 = jnp.float32, jnp.bfloat16, jnp.int32
HIGH = lax.Precision.HIGHEST
STEP = 10.0
MOMENTUM = 0.5
MESH = pl.DeviceIdType.MESH
VMEM = pltpu.VMEM
DMA = pltpu.SemaphoreType.DMA
VM_LIMIT = 60 * 2**20


def nn(a, b, precision=None):
    return lax.dot_general(a, b, (((1,), (0,)), ((), ())), precision=precision, preferred_element_type=f32)


def nt(a, b, precision=None):
    return lax.dot_general(a, b, (((1,), (1,)), ((), ())), precision=precision, preferred_element_type=f32)


def halves(x):
    hi = x.astype(bf16)
    return hi, (x - hi.astype(f32)).astype(bf16)


def nn3(a, b):
    (ah, al), (bh, bl) = halves(a), halves(b)
    return nn(ah, bh) + (nn(ah, bl) + nn(al, bh))


def nt3(a, b):
    (ah, al), (bh, bl) = halves(a), halves(b)
    return nt(ah, bh) + (nt(ah, bl) + nt(al, bh))


def eye(n, m=None):
    m = m or n
    rows = lax.broadcasted_iota(i32, (n, m), 0)
    return (rows == lax.broadcasted_iota(i32, (n, m), 1)).astype(f32)


def chol_inverse(cross):
    n = cross.shape[0]
    both = jnp.concatenate([cross, eye(n)], axis=1)
    tiles = [both[8 * i : 8 * i + 8] for i in range(n // 8)]
    row_id = lax.broadcasted_iota(i32, (8, 1), 0)
    for k in range(n):
        at, sub = k // 8, k % 8
        row = tiles[at][sub : sub + 1]
        row = row / row[:, k : k + 1]
        for i in range(at, n // 8):
            column = tiles[i][:, k : k + 1]
            if i == at:
                column = jnp.where(row_id > sub, column, 0.0)
            tiles[i] = tiles[i] - column * row
    both = jnp.concatenate(tiles, axis=0)
    pivots = jnp.sum(both[:, :n] * eye(n), axis=1, keepdims=True)
    return both[:, n:] * lax.rsqrt(pivots)


def position():
    me = lax.axis_index("curve")
    return me, me // 32, (me // 8) % 4, (me // 2) % 4, me % 2


def partner(k):
    me, y, x, z, c = position()
    dz = (k // 2) % 4
    y, x, z, c = (y + k // 32 + dz) % 4, (x + k // 8 + dz) % 4, (z + dz) % 4, (c + k) % 2
    return ((y * 4 + x) * 4 + z) * 2 + c


def greet_all(n):
    barrier = pltpu.get_barrier_semaphore()

    @pl.loop(1, n)
    def _(k):
        pl.semaphore_signal(barrier, inc=1, device_id=(partner(k),), device_id_type=MESH)

    pl.semaphore_wait(barrier, n - 1)


def send(src, dst, ssem, rsem, to):
    copy = pltpu.make_async_remote_copy(
        src_ref=src, dst_ref=dst, send_sem=ssem, recv_sem=rsem, device_id=(to,), device_id_type=MESH
    )
    copy.start()
    return copy


def drain(ref, sem):
    pltpu.make_async_copy(ref, ref, sem).wait()


class Reduction:
    @staticmethod
    def scratch(rows):
        piece = rows // 8
        return [
            VMEM((8, piece, 128), f32),
            VMEM((8, piece, 128), f32),
            VMEM((4, piece, 128), f32),
            VMEM((4, piece, 128), f32),
            VMEM((8, piece, 128), f32),
            DMA((4,)),
            DMA((4,)),
        ]

    def __init__(self, refs):
        self.src, self.first, self.second, self.third, self.out, self.ss, self.rs = refs
        me, self.y, self.x, _, _ = position()
        self.sub = me % 8
        self.base = me - self.sub

    def peers(self):
        near = [self.base + (self.sub + k) % 8 for k in range(1, 8)]
        across = [((self.y * 4 + (self.x + k) % 4) * 8 + self.sub) for k in range(1, 4)]
        up = [(((self.y + k) % 4 * 4 + self.x) * 8 + self.sub) for k in range(1, 4)]
        return near, across, up

    def start(self, value):
        piece = value.shape[0] // 8
        for i in range(8):
            self.src[i] = value[i * piece : (i + 1) * piece]
        for k in range(1, 8):
            other = (self.sub + k) % 8
            send(self.src.at[other], self.first.at[self.sub], self.ss.at[0], self.rs.at[0], self.base + other)
        self.first[self.sub] = self.src[self.sub]

    def across(self):
        drain(self.first.at[pl.ds(0, 7)], self.rs.at[0])
        total = self.first[0]
        for i in range(1, 8):
            total = total + self.first[i]
        self.second[self.x] = total
        for k in range(1, 4):
            to = (self.y * 4 + (self.x + k) % 4) * 8 + self.sub
            send(self.second.at[self.x], self.second.at[self.x], self.ss.at[1], self.rs.at[1], to)

    def up(self):
        drain(self.second.at[pl.ds(0, 3)], self.rs.at[1])
        self.third[self.y] = (self.second[0] + self.second[1]) + (self.second[2] + self.second[3])
        for k in range(1, 4):
            to = ((self.y + k) % 4 * 4 + self.x) * 8 + self.sub
            send(self.third.at[self.y], self.third.at[self.y], self.ss.at[2], self.rs.at[2], to)

    def gather(self):
        drain(self.third.at[pl.ds(0, 3)], self.rs.at[2])
        self.out[self.sub] = (self.third[0] + self.third[1]) + (self.third[2] + self.third[3])
        for k in range(1, 8):
            send(
                self.out.at[self.sub],
                self.out.at[self.sub],
                self.ss.at[3],
                self.rs.at[3],
                self.base + (self.sub + k) % 8,
            )

    def result(self):
        drain(self.out.at[pl.ds(0, 7)], self.rs.at[3])
        drain(self.src.at[pl.ds(0, 7)], self.ss.at[0])
        drain(self.second.at[pl.ds(0, 3)], self.ss.at[1])
        drain(self.third.at[pl.ds(0, 3)], self.ss.at[2])
        drain(self.out.at[pl.ds(0, 7)], self.ss.at[3])
        return jnp.concatenate([self.out[i] for i in range(8)], axis=0)


def block(b):
    return pl.ds(pl.multiple_of(b * 128, 128), 128)


def start_kernel(
    n, rb, bands, points,
    far_row, send_slot, panel, diag_hbm, super_hbm, far_hbm,
    x_out, v_out, root_out,
    diag, sup, far, deg, far_sums, cols, cols_in, tail_in, load_sem, small_sem,
    *reduction,
):
    width = panel.shape[0]
    slots = far.shape[0]
    loads = [
        pltpu.make_async_copy(diag_hbm, diag, load_sem.at[0]),
        pltpu.make_async_copy(super_hbm, sup, load_sem.at[1]),
        pltpu.make_async_copy(far_hbm, far, load_sem.at[2]),
    ]
    for load in loads:
        load.start()
    greet_all(n)
    total = Reduction(reduction)
    me = lax.axis_index("curve")

    hi, lo = halves(panel[...])
    cross = nt(hi, lo)
    gram = nt(hi, hi) + (cross + cross.T)
    total.start(jnp.concatenate([gram, jnp.zeros_like(gram)], axis=1))

    deg[...] = jnp.zeros_like(deg)
    ones = jnp.ones((16, 128), bf16)
    for load in loads[:2]:
        load.wait()

    def near(b, carry):
        rows = nt(ones, diag[b])[0:1] + nn(ones, diag[b])[0:1]
        for h in range(bands):
            rows = rows + nt(ones, sup[b, h])[0:1]
            deg[pl.ds(b + h + 1, 1), :] += nn(ones, sup[b, h])[0:1]
        deg[pl.ds(b, 1), :] += rows
        return carry

    lax.fori_loop(0, rb // 2, near, 0)
    total.across()
    lax.fori_loop(rb // 2, rb, near, 0)
    total.up()
    following = (me + 1) % n
    tail = send(deg.at[pl.ds(rb, 8)], tail_in, small_sem.at[0], small_sem.at[1], following)
    loads[2].wait()
    sub = lax.broadcasted_iota(i32, (8, 128), 0)

    def far_one(k, carry):
        t = partner(k)
        pair = []
        for c in range(2):
            f = 2 * t + c
            far_sums[pl.ds(f, 1), :] = nt(ones, far[f])[0:1]
            pair.append(nn(ones, far[f])[0:1])
        cols[t] = jnp.where(sub == 0, pair[0], jnp.where(sub == 1, pair[1], 0.0))
        return carry

    far_one(0, 0)
    cols_in[me] = cols[me]

    def far_step(k, carry):
        far_one(k, carry)
        t = partner(k)
        send(cols.at[t], cols_in.at[me], small_sem.at[2], small_sem.at[3], t)
        return carry

    lax.fori_loop(1, n // 2, far_step, 0)
    total.gather()
    lax.fori_loop(n // 2, n, far_step, 0)

    inverse = chol_inverse(total.result()[:, :width] * (1.0 / points))
    x0 = nn3(inverse, panel[...])
    x_out[...] = x0

    owner_rows = lax.broadcasted_iota(i32, (rb, slots), 0)
    degree = deg[0:rb, :] + nn((owner_rows == far_row[...]).astype(f32), far_sums[...], HIGH)
    tail.wait_recv()
    degree = degree + jnp.concatenate([tail_in[...], jnp.zeros((rb - 8, 128), f32)], axis=0)
    drain(cols_in.at[pl.ds(0, n - 1)], small_sem.at[3])
    slot_rows = lax.broadcasted_iota(i32, (rb, 8 * n), 0)
    degree = degree + nn((slot_rows == send_slot[...]).astype(f32), cols_in[...].reshape(8 * n, 128), HIGH)
    root = lax.rsqrt(degree)
    root_out[...] = root
    for b in range(rb):
        lanes = slice(b * 128, b * 128 + 128)
        v_out[b] = (x0[:, lanes] * root[b : b + 1]).astype(bf16)
    tail.wait_send()
    drain(cols.at[pl.ds(0, n - 1)], small_sem.at[2])


def start(n, diag_blocks, super_blocks, far_blocks, far_row, send_slot, panel):
    rb, bs = diag_blocks.shape[:2]
    bands, slots, width = super_blocks.shape[1], far_blocks.shape[0], panel.shape[0]
    owned = rb * bs
    send_pad = jnp.pad(send_slot.reshape(n, 2), ((0, 0), (0, 6)), constant_values=-1).reshape(1, 8 * n)
    here = pl.BlockSpec(memory_space=pltpu.VMEM)
    away = pl.BlockSpec(memory_space=pl.ANY)
    return pl.pallas_call(
        functools.partial(start_kernel, n, rb, bands, float(n * owned)),
        out_shape=(
            jax.ShapeDtypeStruct((width, owned), f32),
            jax.ShapeDtypeStruct((rb, width, bs), bf16),
            jax.ShapeDtypeStruct((rb, bs), f32),
        ),
        in_specs=[here, here, here, away, away, away],
        out_specs=(here, here, here),
        scratch_shapes=[
            VMEM(diag_blocks.shape, bf16),
            VMEM(super_blocks.shape, bf16),
            VMEM(far_blocks.shape, bf16),
            VMEM((rb + 8, bs), f32),
            VMEM((slots, bs), f32),
            VMEM((n, 8, bs), f32),
            VMEM((n, 8, bs), f32),
            VMEM((8, bs), f32),
            DMA((3,)),
            DMA((4,)),
            *Reduction.scratch(width),
        ],
        compiler_params=pltpu.CompilerParams(collective_id=1, has_side_effects=True, vmem_limit_bytes=VM_LIMIT),
        name="start",
    )(far_row.reshape(1, slots), send_pad, panel, diag_blocks, super_blocks, far_blocks)


def exchange_kernel(
    n, rb, bands, last,
    index, keep, v, root, diag_hbm, super_hbm, far_hbm, *rest,
):
    if last:
        x_hbm, prev_hbm, t_out, gram_out, *rest = rest
    else:
        t_out, u_out, *rest = rest
    diag, sup, far, ahead, near, stage, mirror, came, back, seg, tail_in, load_sem, sems, *rest = rest
    width, owned = v.shape[1], rb * 128
    slots = far.shape[0]
    me = lax.axis_index("curve")
    loads = [
        pltpu.make_async_copy(far_hbm, far, load_sem.at[0]),
        pltpu.make_async_copy(diag_hbm, diag, load_sem.at[1]),
        pltpu.make_async_copy(super_hbm, sup, load_sem.at[2]),
    ]
    if last:
        x0, prev = rest
        loads += [
            pltpu.make_async_copy(x_hbm, x0, load_sem.at[3]),
            pltpu.make_async_copy(prev_hbm, prev, load_sem.at[4]),
        ]
    for load in loads:
        load.start()
    greet_all(n)
    halo = send(
        v.at[pl.ds(0, bands)], ahead, sems.at[0], sems.at[1], (me + n - 1) % n
    )

    def stage_one(k):
        t = partner(k)
        for c in range(2):
            stage[2 * t + c] = v[index[0, 2 * t + c]]
        return t

    stage_one(0)
    came[pl.ds(2 * me, 2)] = stage[pl.ds(2 * me, 2)]

    def stage_step(k, carry):
        t = stage_one(k)
        send(stage.at[pl.ds(2 * t, 2)], came.at[pl.ds(2 * me, 2)], sems.at[2], sems.at[3], t)
        return carry

    lax.fori_loop(1, n, stage_step, 0)
    loads[0].wait()

    def mirror_one(k):
        t = partner(k)
        for c in range(2):
            f = 2 * t + c
            mirror[f] = nn(v[index[1, f]], far[f]).astype(bf16)
        return t

    mirror_one(0)
    back[pl.ds(2 * me, 2)] = mirror[pl.ds(2 * me, 2)]

    def mirror_step(k, carry):
        t = mirror_one(k)
        send(mirror.at[pl.ds(2 * t, 2)], back.at[pl.ds(2 * me, 2)], sems.at[4], sems.at[5], t)
        return carry

    lax.fori_loop(1, n, mirror_step, 0)

    near[...] = jnp.zeros_like(near)
    loads[1].wait()
    loads[2].wait()

    def near_one(b, fetch):
        vb = v[b]
        out = nt(vb, diag[b]) + nn(vb, diag[b])
        for h in range(bands):
            out = out + nt(fetch(b, h), sup[b, h])
            near[:, block(b + h + 1)] += nn(vb, sup[b, h])
        near[:, block(b)] += out

    def near_step(b, carry):
        near_one(b, lambda b, h: v[b + h + 1])
        return carry

    lax.fori_loop(0, rb - bands, near_step, 0)
    halo.wait_recv()
    for b in range(rb - bands, rb):

        def fetch(b, h):
            at = b + h + 1
            return v[at] if at < rb else ahead[at - rb]

        near_one(b, fetch)
    tail = send(
        near.at[:, pl.ds(owned, bands * 128)], tail_in, sems.at[6], sems.at[7], (me + 1) % n
    )
    if last:
        for load in loads[3:]:
            load.wait()
        (xh, xl), (ph, pl_) = halves(x0[...]), halves(prev[...])
        gram_out[0:width, 0:width] = nt(xh, ph) + (nt(xh, pl_) + nt(xl, ph))
        cross = nt(ph, pl_)
        gram_out[0:width, width : 2 * width] = nt(ph, ph) + (cross + cross.T)
        cross = nt(xh, xl)
        gram_out[2 * width : 3 * width, width : 2 * width] = nt(xh, xh) + (cross + cross.T)

    drain(came.at[pl.ds(0, slots - 2)], sems.at[3])
    zero = jnp.zeros((width, 128), f32)

    def forward(j4, total):
        for i in range(4):
            j = j4 * 4 + i
            f = index[2, j]
            total = total * keep[0, j] + nt(came[f], far[f])
            seg[j] = total
        return total

    lax.fori_loop(0, slots // 4, forward, zero)

    def add_forward(b, carry):
        near[:, block(b)] += seg[index[4, b]] * keep[2, b]
        return carry

    lax.fori_loop(0, rb, add_forward, 0)
    tail.wait_recv()
    near[:, 0 : bands * 128] += tail_in[...]

    drain(back.at[pl.ds(0, slots - 2)], sems.at[5])

    def backward(j4, total):
        for i in range(4):
            j = j4 * 4 + i
            total = total * keep[1, j] + back[index[3, j]].astype(f32)
            seg[j] = total
        return total

    lax.fori_loop(0, slots // 4, backward, zero)

    def finish(b, carry):
        d = root[pl.ds(b, 1), :]
        t = (near[:, block(b)] + seg[index[5, b]] * keep[3, b]) * d
        t_out[:, block(b)] = t
        if not last:
            u_out[b] = (t * d).astype(bf16)
        return carry

    lax.fori_loop(0, rb, finish, 0)
    if last:
        th, tl = halves(t_out[...])
        gram_out[width : 2 * width, 0:width] = nt(xh, th) + (nt(xh, tl) + nt(xl, th))
        gram_out[width : 2 * width, width : 2 * width] = nt(ph, th) + (nt(ph, tl) + nt(pl_, th))
        cross = nt(th, tl)
        gram_out[2 * width : 3 * width, 0:width] = nt(th, th) + (cross + cross.T)
    halo.wait_send()
    tail.wait_send()
    drain(stage.at[pl.ds(0, slots - 2)], sems.at[2])
    drain(mirror.at[pl.ds(0, slots - 2)], sems.at[4])


def exchange(n, tables, v, root, diag_blocks, super_blocks, far_blocks, extra):
    rb, bs = diag_blocks.shape[:2]
    bands, slots = super_blocks.shape[1], far_blocks.shape[0]
    width, owned = v.shape[1], rb * bs
    last = bool(extra)
    here = pl.BlockSpec(memory_space=pltpu.VMEM)
    away = pl.BlockSpec(memory_space=pl.ANY)
    scalar = pl.BlockSpec(memory_space=pltpu.SMEM)
    outs = [jax.ShapeDtypeStruct((width, owned), f32)]
    outs.append(
        jax.ShapeDtypeStruct((3 * width, 2 * width), f32) if last else jax.ShapeDtypeStruct((rb, width, bs), bf16)
    )
    return pl.pallas_call(
        functools.partial(exchange_kernel, n, rb, bands, last),
        out_shape=tuple(outs),
        in_specs=[scalar, scalar, here, here, away, away, away] + [away] * len(extra),
        out_specs=(here, here),
        scratch_shapes=[
            VMEM(diag_blocks.shape, bf16),
            VMEM(super_blocks.shape, bf16),
            VMEM(far_blocks.shape, bf16),
            VMEM((bands, width, bs), bf16),
            VMEM((width, owned + bands * bs), f32),
            VMEM((slots, width, bs), bf16),
            VMEM((slots, width, bs), bf16),
            VMEM((slots, width, bs), bf16),
            VMEM((slots, width, bs), bf16),
            VMEM((slots, width, bs), f32),
            VMEM((width, bands * bs), f32),
            DMA((3 + len(extra),)),
            DMA((8,)),
            *[VMEM((width, owned), f32) for _ in extra],
        ],
        compiler_params=pltpu.CompilerParams(
            collective_id=3 if last else 2, has_side_effects=True, vmem_limit_bytes=VM_LIMIT
        ),
        name="last_exchange" if last else "first_exchange",
    )(*tables, v, root, diag_blocks, super_blocks, far_blocks, *extra)


def small_kernel(points, gram, coef, *reduction):
    barrier = pltpu.get_barrier_semaphore()
    total = Reduction(reduction)
    near, across, up = total.peers()
    for to in near + across + up:
        pl.semaphore_signal(barrier, inc=1, device_id=(to,), device_id_type=MESH)
    pl.semaphore_wait(barrier, 13)
    total.start(gram[...])
    total.across()
    total.up()
    total.gather()
    w = gram.shape[1] // 2
    sums = total.result() * (1.0 / points)
    h01, h11 = sums[0:w, 0:w], sums[0:w, w:]
    h02, h12 = sums[w : 2 * w, 0:w], sums[w : 2 * w, w:]
    h22, h00 = sums[2 * w :, 0:w], sums[2 * w :, w:]
    mul = functools.partial(nn, precision=HIGH)
    mul_t = functools.partial(nt, precision=HIGH)
    one = eye(w)
    y0 = one - STEP * h01.T
    part = mul(y0, h01)
    m1 = chol_inverse(mul_t(mul(y0, h00), y0) + STEP * (part + part.T) + STEP * STEP * h11)
    a0, a1 = mul(m1, y0), STEP * m1
    s01 = mul_t(h01, a0) + mul_t(h02, a1)
    s11 = mul_t(h11, a0) + mul_t(h12, a1)
    rayleigh = mul(a0, s01) + mul(a1, s11)
    turn = one - STEP * rayleigh.T
    b0 = mul(turn, a0) + MOMENTUM * (a0 - one)
    b1 = mul(turn, a1) + STEP * a0 + MOMENTUM * a1
    b2 = STEP * a1
    p01, p02, p12 = mul(b0, mul_t(h01, b1)), mul(b0, mul_t(h02, b2)), mul(b1, mul_t(h12, b2))
    mixed = p01 + p02 + p12
    square = mul(b0, mul_t(h00, b0)) + mul(b1, mul_t(h11, b1)) + mul(b2, mul_t(h22, b2))
    m2 = chol_inverse(square + (mixed + mixed.T))
    c0, c1, c2 = mul(m2, b0), mul(m2, b1), mul(m2, b2)
    coef[...] = jnp.zeros_like(coef)
    coef[0:w, 0:w] = c0
    coef[0:w, w : 2 * w] = c1
    coef[0:w, 2 * w : 3 * w] = c2
    coef[w:, 0:w] = c0 - a0
    coef[w:, w : 2 * w] = c1 - a1
    coef[w:, 2 * w : 3 * w] = c2


def small(points, gram):
    w = gram.shape[1] // 2
    here = pl.BlockSpec(memory_space=pltpu.VMEM)
    return pl.pallas_call(
        functools.partial(small_kernel, points),
        out_shape=jax.ShapeDtypeStruct((2 * w, 4 * w), f32),
        in_specs=[here],
        out_specs=here,
        scratch_shapes=Reduction.scratch(gram.shape[0]),
        compiler_params=pltpu.CompilerParams(collective_id=4, has_side_effects=True, vmem_limit_bytes=VM_LIMIT),
        name="small",
    )(gram)


def combine_kernel(coef, x0, t1, t2, basis, update):
    w = x0.shape[0]
    out = nn3(coef[:, 0 : 3 * w], jnp.concatenate([x0[...], t1[...], t2[...]], axis=0))
    basis[...] = out[:w]
    update[...] = out[w:]


def combine(coef, x0, t1, t2):
    w, owned = x0.shape
    chunk = 2048
    panel = pl.BlockSpec((w, chunk), lambda i: (0, i))
    return pl.pallas_call(
        combine_kernel,
        grid=(owned // chunk,),
        out_shape=(jax.ShapeDtypeStruct((w, owned), f32),) * 2,
        in_specs=[pl.BlockSpec(coef.shape, lambda i: (0, 0)), panel, panel, panel],
        out_specs=(panel, panel),
        compiler_params=pltpu.CompilerParams(vmem_limit_bytes=VM_LIMIT),
        name="combine",
    )(coef, x0, t1, t2)


def segments(key, rb):
    slots = key.shape[0]
    at = jnp.arange(slots, dtype=i32)
    mixed = key * slots + at
    rank = jnp.sum((mixed[None, :] < mixed[:, None]).astype(i32), axis=1)
    hit = (rank[None, :] == at[:, None]).astype(i32)
    order = jnp.sum(hit * at[None, :], axis=1)
    ranked = jnp.sum(hit * key[None, :], axis=1)
    before = jnp.concatenate([jnp.full((1,), -2, i32), ranked[:-1]])
    row = jnp.arange(rb, dtype=i32)
    last = jnp.sum((key[None, :] <= row[:, None]).astype(i32), axis=1) - 1
    any_here = jnp.max((key[None, :] == row[:, None]).astype(f32), axis=1)
    return order, (ranked == before).astype(f32), jnp.maximum(last, 0), any_here


def shards(diag_blocks, super_blocks, far_blocks, far_row, send_slot, panel):
    n = lax.axis_size("curve")
    rb, bs = diag_blocks.shape[:2]
    points = float(n * rb * bs)
    slots = far_row.shape[0]
    f_order, f_keep, f_last, f_any = segments(far_row, rb)
    s_order, s_keep, s_last, s_any = segments(send_slot, rb)

    def wide(x):
        return jnp.pad(x, (0, slots - x.shape[0]))

    index = jnp.stack(
        [jnp.maximum(send_slot, 0), jnp.maximum(far_row, 0), f_order, s_order, wide(f_last), wide(s_last)]
    )
    keep = jnp.stack([f_keep, s_keep, wide(f_any), wide(s_any)])
    x0, v0, root = start(n, diag_blocks, super_blocks, far_blocks, far_row, send_slot, panel)
    blocks = (diag_blocks, super_blocks, far_blocks)
    t1, u = exchange(n, (index, keep), v0, root, *blocks, ())
    t2, gram = exchange(n, (index, keep), u, root, *blocks, (x0, t1))
    return combine(small(points, gram), x0, t1, t2)


def solution(mesh):
    return jax.shard_map(
        shards,
        mesh=mesh,
        in_specs=(
            P("curve", None, None),
            P("curve", None, None, None),
            P("curve", None, None),
            P("curve"),
            P("curve"),
            P(None, "curve"),
        ),
        out_specs=(P(None, "curve"), P(None, "curve")),
        check_vma=False,
    )
```

time: 962 us -> 352 us (0.37)
  Pallas kernels: 0 us -> 342 us
  blocking collectives: 326 us -> 0 us
  matrix products: 189 us -> 0 us
  other arithmetic: 196 us -> 7.26 us
  waiting for transfers between devices: 130 us -> 0 us
  starting transfers between devices: 59.2 us -> 0 us
  local copies, waits for them, and re-layouts: 50.7 us -> 2.15 us
    pallas_call x0 -> x5, Pallas kernels: none -> 342 us  [the longest x2 234 us: exchange(): pl.pallas_call(functools.partial(exchange_kernel, n, rb, bands, last), ou...]
    psum x5 -> x0, blocking collectives: 326 us -> none  [the longest x2 134 us: shards(): rayleigh = lax.psum(gram_of(current, image), 'curve') / total_points]
    dot_general x46 -> x0, matrix products: 188 us -> none  [the longest x12 42.3 us: near_apply(): jnp.einsum('bcp,bpq->bcq', behind, supers_ext[first:first + rows_dev, ban...]
    scatter-add x6 -> x0, other arithmetic: 135 us -> none  [the longest x3 67.6 us: apply_w(): result = result.at[send_index].add(jnp.where(send_live, returned, 0.0))]
    all_to_all x6 -> x0, waiting for transfers between devices: 130 us -> none  [the longest x3 76.9 us: apply_w(): lax.all_to_all(mirror, 'curve', split_axis=0, concat_axis=0, tiled=True)]
    all_to_all x6 -> x0, starting transfers between devices: 51.4 us -> none  [the longest x3 32.9 us: apply_w(): lax.all_to_all(outgoing, 'curve', split_axis=0, concat_axis=0, tiled=True)]
    another operation x15 -> x1, other arithmetic: 36.2 us -> 0.61 us  [shards(): keep = jnp.stack([f_keep, s_keep, wide(f_any), wide(s_any)])]
    select_n x6 -> x0, other arithmetic: 21 us -> none  [the longest x2 12.1 us: apply_w(): result = result.at[send_index].add(jnp.where(send_live, returned, 0.0))]
  transfers between devices with their start and end apart: 13 -> 0, of which waited for: 4 -> 0; matrix products, arithmetic and copies ran while one was open for 28% -> 0% of each run, Pallas kernels for 0% -> 0%
where the time goes in v1:
time: 352 us
  Pallas kernels  342 us (97%)
  other arithmetic  7.26 us (2%)
    pallas_call x2, Pallas kernels, exchange(): pl.pallas_call(functools.partial(exchange_kernel, n, rb, bands, last), ou...  234 us
    pallas_call x1, Pallas kernels, start(): pl.pallas_call(functools.partial(start_kernel, n, rb, bands, float(n * ow...  65.2 us
    pallas_call x1, Pallas kernels, small(): pl.pallas_call(functools.partial(small_kernel, points), out_shape=jax.Sha...  36.2 us

profile of v1, /device:TPU:1, one launch (start us, length us, event | category | flops | bytes accessed | tf_op | source)
XLA Modules:
  0.0 351.8 jit_solution(897704793039672292)
XLA Ops:
  0.6 0.8 convert_reduce_fusion.5
  1.4 0.8 convert_reduce_fusion.3
  2.2 0.8 convert_reduce_fusion.4
  3.1 0.8 convert_reduce_fusion.2
  3.9 0.7 iota_add_fusion.1
  4.6 0.2 convert_reduce_fusion.1
  4.7 0.8 select_reduce_fusion.1
  5.6 0.7 iota_add_fusion
  6.3 0.2 convert_reduce_fusion
  6.4 0.8 select_reduce_fusion
  7.3 0.1 compare_convert_fusion
  7.4 0.6 pad_maximum_fusion.keep
  8.0 0.6 stack.38.index
  8.6 0.8 reshape.85
  9.4 0.7 reshape.86.send_slot
  10.1 65.2 %start.1 = (f32[64,8192]{1,0:T(8,128)}, bf16[64,64,128]{2,1,0:T(8,128)(2,1)}, f32[64,128]{1,0:T(8,128)}) custom-call(s32[1,256]{1,0:T(1,128)} %bitcast.15, s32[1,1024]{1,0:T(1,128)} %reshape.86.send_slot, f32[64,8192]{1,0:T(8,128)} %panel.1, bf16[64,128,128]{2,1,0:T(8,128)(2,1)} %diag_hbm.5, bf16[64,4,128,128]{3,2,1,0:T(8,128)(2,1)} %super_hbm.5, ...), custom_call_target="tpu_custom_call" | custom-call | tf_op jit(solution)/shard_map/start/pallas_call | solution.py:276
  75.3 115.0 %first_exchange.1 = (f32[64,8192]{1,0:T(8,128)}, bf16[64,64,128]{2,1,0:T(8,128)(2,1)}) custom-call(s32[6,256]{1,0:T(8,128)} %stack.38.index, f32[4,256]{1,0:T(4,128)} %pad_maximum_fusion.keep, bf16[64,64,128]{2,1,0:T(8,128)(2,1)} %get-tuple-element.9.v, f32[64,128]{1,0:T(8,128)} %get-tuple-element.10.root, bf16[64,128,128]{2,1,0:T(8,128)(2,1)} %diag_hbm.5, ...), custom_call_target="tpu_custom_call" | custom-call | tf_op jit(solution)/shard_map/first_exchange/pallas_call | solution.py:470
  190.3 119.0 %last_exchange.1 = (f32[64,8192]{1,0:T(8,128)}, f32[192,128]{1,0:T(8,128)}) custom-call(s32[6,256]{1,0:T(8,128)} %stack.38.index, f32[4,256]{1,0:T(4,128)} %pad_maximum_fusion.keep, bf16[64,64,128]{2,1,0:T(8,128)(2,1)} %get-tuple-element.11.v, f32[64,128]{1,0:T(8,128)} %get-tuple-element.10.root, bf16[64,128,128]{2,1,0:T(8,128)(2,1)} %diag_hbm.5, ...), custom_call_target="tpu_custom_call" | custom-call | tf_op jit(solution)/shard_map/last_exchange/pallas_call | solution.py:470
  309.2 36.2 %small.1.coef = f32[128,256]{1,0:T(8,128)} custom-call(f32[192,128]{1,0:T(8,128)} %get-tuple-element.14.gram), custom_call_target="tpu_custom_call" | custom-call | tf_op jit(solution)/shard_map/small/pallas_call | solution.py:545
  345.4 6.4 %combine.1 = (f32[64,8192]{1,0:T(8,128)}, f32[64,8192]{1,0:T(8,128)}) custom-call(f32[128,256]{1,0:T(8,128)} %small.1.coef, f32[64,8192]{1,0:T(8,128)} %get-tuple-element.12.rest_0_.x0, f32[64,8192]{1,0:T(8,128)} %get-tuple-element.13.rest_1_.t1, f32[64,8192]{1,0:T(8,128)} %get-tuple-element.15.t2), custom_call_target="tpu_custom_call" | custom-call | tf_op jit(solution)/shard_map/combine/pallas_call | solution.py:567
  (7 shorter events, 0.0 us)

commit v2 on v0

v2 whole, which is shorter than its diff:
```python
import functools

import jax
import jax.numpy as jnp
from jax import lax
from jax.experimental import pallas as pl
from jax.experimental.pallas import tpu as pltpu
from jax.sharding import PartitionSpec as P

f32, bf16, i32 = jnp.float32, jnp.bfloat16, jnp.int32
HIGH = lax.Precision.HIGHEST
STEP = 10.0
MOMENTUM = 0.5
MESH = pl.DeviceIdType.MESH
VMEM = pltpu.VMEM
DMA = pltpu.SemaphoreType.DMA
VM_LIMIT = 62 * 2**20


def nn(a, b, precision=None):
    return lax.dot_general(a, b, (((1,), (0,)), ((), ())), precision=precision, preferred_element_type=f32)


def nt(a, b, precision=None):
    return lax.dot_general(a, b, (((1,), (1,)), ((), ())), precision=precision, preferred_element_type=f32)


def halves(x):
    hi = x.astype(bf16)
    return hi, (x - hi.astype(f32)).astype(bf16)


def nn3(a, b):
    (ah, al), (bh, bl) = halves(a), halves(b)
    return nn(ah, bh) + (nn(ah, bl) + nn(al, bh))


def nt3(a, b):
    (ah, al), (bh, bl) = halves(a), halves(b)
    return nt(ah, bh) + (nt(ah, bl) + nt(al, bh))


def eye(n, m=None):
    m = m or n
    rows = lax.broadcasted_iota(i32, (n, m), 0)
    return (rows == lax.broadcasted_iota(i32, (n, m), 1)).astype(f32)


def chol_inverse(cross):
    n = cross.shape[0]
    both = jnp.concatenate([cross, eye(n)], axis=1)
    tiles = [both[8 * i : 8 * i + 8] for i in range(n // 8)]
    row_id = lax.broadcasted_iota(i32, (8, 1), 0)
    for k in range(n):
        at, sub = k // 8, k % 8
        row = tiles[at][sub : sub + 1]
        row = row / row[:, k : k + 1]
        for i in range(at, n // 8):
            column = tiles[i][:, k : k + 1]
            if i == at:
                column = jnp.where(row_id > sub, column, 0.0)
            tiles[i] = tiles[i] - column * row
    both = jnp.concatenate(tiles, axis=0)
    pivots = jnp.sum(both[:, :n] * eye(n), axis=1, keepdims=True)
    return both[:, n:] * lax.rsqrt(pivots)


def position():
    me = lax.axis_index("curve")
    return me, me // 32, (me // 8) % 4, (me // 2) % 4, me % 2


def partner(k):
    me, y, x, z, c = position()
    dz = (k // 2) % 4
    y, x, z, c = (y + k // 32 + dz) % 4, (x + k // 8 + dz) % 4, (z + dz) % 4, (c + k) % 2
    return ((y * 4 + x) * 4 + z) * 2 + c


def send(src, dst, ssem, rsem, to):
    copy = pltpu.make_async_remote_copy(
        src_ref=src, dst_ref=dst, send_sem=ssem, recv_sem=rsem, device_id=(to,), device_id_type=MESH
    )
    copy.start()
    return copy


def drain(ref, sem):
    pltpu.make_async_copy(ref, ref, sem).wait()


class Reduction:
    @staticmethod
    def scratch(rows):
        piece = rows // 8
        return [
            VMEM((8, piece, 128), f32),
            VMEM((8, piece, 128), f32),
            VMEM((16, piece, 128), f32),
            VMEM((8, piece, 128), f32),
            DMA((3,)),
            DMA((3,)),
        ]

    def __init__(self, refs):
        self.src, self.first, self.second, self.out, self.ss, self.rs = refs
        me = lax.axis_index("curve")
        self.sub = me % 8
        self.plane = me // 8

    def start(self, value):
        piece = value.shape[0] // 8
        for i in range(8):
            self.src[i] = value[i * piece : (i + 1) * piece]
        for k in range(1, 8):
            other = (self.sub + k) % 8
            send(self.src.at[other], self.first.at[self.sub], self.ss.at[0], self.rs.at[0], self.plane * 8 + other)
        self.first[self.sub] = self.src[self.sub]

    def across(self):
        drain(self.first.at[pl.ds(0, 7)], self.rs.at[0])
        total = self.first[0]
        for i in range(1, 8):
            total = total + self.first[i]
        self.second[self.plane] = total
        for k in range(1, 16):
            to = (self.plane + k) % 16 * 8 + self.sub
            send(self.second.at[self.plane], self.second.at[self.plane], self.ss.at[1], self.rs.at[1], to)

    def gather(self):
        drain(self.second.at[pl.ds(0, 15)], self.rs.at[1])
        parts = [self.second[i] for i in range(16)]
        while len(parts) > 1:
            parts = [a + b for a, b in zip(parts[::2], parts[1::2])]
        self.out[self.sub] = parts[0]
        for k in range(1, 8):
            to = self.plane * 8 + (self.sub + k) % 8
            send(self.out.at[self.sub], self.out.at[self.sub], self.ss.at[2], self.rs.at[2], to)

    def result(self):
        drain(self.out.at[pl.ds(0, 7)], self.rs.at[2])
        return jnp.concatenate([self.out[i] for i in range(8)], axis=0)

    def close(self):
        drain(self.src.at[pl.ds(0, 7)], self.ss.at[0])
        drain(self.second.at[pl.ds(0, 15)], self.ss.at[1])
        drain(self.out.at[pl.ds(0, 7)], self.ss.at[2])


def block(b):
    return pl.ds(pl.multiple_of(b * 128, 128), 128)


GROUPS = 4


def coefficients(gram, w):
    h01, h11 = gram[0:w, 0:w], gram[0:w, w:]
    h02, h12 = gram[w : 2 * w, 0:w], gram[w : 2 * w, w:]
    h22, h00 = gram[2 * w :, 0:w], gram[2 * w :, w:]
    mul = functools.partial(nn, precision=HIGH)
    mul_t = functools.partial(nt, precision=HIGH)
    one = eye(w)
    y0 = one - STEP * h01.T
    part = mul(y0, h01)
    m1 = chol_inverse(mul_t(mul(y0, h00), y0) + STEP * (part + part.T) + STEP * STEP * h11)
    a0, a1 = mul(m1, y0), STEP * m1
    s01 = mul_t(h01, a0) + mul_t(h02, a1)
    s11 = mul_t(h11, a0) + mul_t(h12, a1)
    rayleigh = mul(a0, s01) + mul(a1, s11)
    turn = one - STEP * rayleigh.T
    b0 = mul(turn, a0) + MOMENTUM * (a0 - one)
    b1 = mul(turn, a1) + STEP * a0 + MOMENTUM * a1
    b2 = STEP * a1
    p01, p02, p12 = mul(b0, mul_t(h01, b1)), mul(b0, mul_t(h02, b2)), mul(b1, mul_t(h12, b2))
    mixed = p01 + p02 + p12
    square = mul(b0, mul_t(h00, b0)) + mul(b1, mul_t(h11, b1)) + mul(b2, mul_t(h22, b2))
    m2 = chol_inverse(square + (mixed + mixed.T))
    c0, c1, c2 = mul(m2, b0), mul(m2, b1), mul(m2, b2)
    return (c0, c1, c2), (c0 - a0, c1 - a1, c2)


def whole_kernel(
    n, rb, bands, points,
    index, keep, index_v, spread, panel_hbm, diag_hbm, super_hbm, far_hbm,
    x_hbm, t1_hbm, t2_hbm, coef,
    diag, sup, far, x0, t1, t2, v, u, root, ahead, near, stage, mirror, seg, tails,
    deg, far_sums, cols, cols_in, deg_tail, load_sem, out_sem, small_sem, send_sem, recv_sem, *rest,
):
    width = x0.shape[0]
    slots = far.shape[0]
    part = slots // GROUPS
    owned = rb * 128
    per = n // GROUPS
    me = lax.axis_index("curve")
    panel = t2
    loads = [
        pltpu.make_async_copy(panel_hbm, panel, load_sem.at[0]),
        pltpu.make_async_copy(diag_hbm, diag, load_sem.at[1]),
        pltpu.make_async_copy(super_hbm, sup, load_sem.at[2]),
        pltpu.make_async_copy(far_hbm, far, load_sem.at[3]),
    ]
    for load in loads:
        load.start()
    barrier = pltpu.get_barrier_semaphore()

    @pl.loop(1, n)
    def _(k):
        pl.semaphore_signal(barrier, inc=1, device_id=(partner(k),), device_id_type=MESH)

    arrive, reductions = rest[: 4 * GROUPS], rest[4 * GROUPS :]
    came1, back1, came2, back2 = (arrive[i * GROUPS : (i + 1) * GROUPS] for i in range(4))
    first_sum, last_sum = Reduction(reductions[:6]), Reduction(reductions[6:])
    following, previous = (me + 1) % n, (me + n - 1) % n

    loads[0].wait()
    hi, lo = halves(panel[...])
    cross = nt(hi, lo)
    gram = nt(hi, hi) + (cross + cross.T)
    deg[...] = jnp.zeros_like(deg)
    ones = jnp.ones((16, 128), bf16)

    def row_sums(blk):
        return nt(ones, blk)[0:1]

    def column_sums(blk):
        return jnp.sum(blk.astype(f32), axis=0, keepdims=True)

    def near_degree(b, carry):
        rows = row_sums(diag[b]) + column_sums(diag[b])
        for h in range(bands):
            rows = rows + row_sums(sup[b, h])
            deg[pl.ds(b + h + 1, 1), :] += column_sums(sup[b, h])
        deg[pl.ds(b, 1), :] += rows
        return carry

    loads[1].wait()
    loads[2].wait()
    lax.fori_loop(0, rb // 2, near_degree, 0)
    pl.semaphore_wait(barrier, n - 1)
    first_sum.start(jnp.concatenate([gram, jnp.zeros_like(gram)], axis=1))
    lax.fori_loop(rb // 2, rb, near_degree, 0)
    first_sum.across()
    deg_sent = send(deg.at[pl.ds(rb, 8)], deg_tail, small_sem.at[0], small_sem.at[1], following)
    loads[3].wait()
    sub = lax.broadcasted_iota(i32, (8, 128), 0)

    def far_degree(k):
        t = partner(k)
        pair = []
        for c in range(2):
            f = 2 * t + c
            far_sums[pl.ds(f, 1), :] = row_sums(far[f])
            pair.append(column_sums(far[f]))
        cols[t] = jnp.where(sub == 0, pair[0], jnp.where(sub == 1, pair[1], 0.0))
        return t

    def far_step(k, carry):
        t = far_degree(k)
        send(cols.at[t], cols_in.at[me], small_sem.at[2], small_sem.at[3], t)
        return carry

    far_degree(0)
    cols_in[me] = cols[me]
    lax.fori_loop(1, n // 2, far_step, 0)
    first_sum.gather()
    lax.fori_loop(n // 2, n, far_step, 0)

    inverse = chol_inverse(first_sum.result()[:, :width] * (1.0 / points))
    x0[...] = nn3(inverse, panel[...])
    saves = [pltpu.make_async_copy(x0, x_hbm, out_sem.at[0])]
    saves[0].start()

    owner_rows = lax.broadcasted_iota(i32, (rb, slots), 0)
    degree = deg[0:rb, :] + nn((owner_rows == index_v[6:7, :]).astype(f32), far_sums[...], HIGH)
    deg_sent.wait_recv()
    degree = degree + jnp.concatenate([deg_tail[...], jnp.zeros((rb - 8, 128), f32)], axis=0)
    slot_rows = lax.broadcasted_iota(i32, (rb, 8 * n), 0)
    chosen = (slot_rows == spread[0:1, :]).astype(f32)
    drain(cols_in.at[pl.ds(0, n - 1)], small_sem.at[3])
    degree = degree + nn(chosen, cols_in[...].reshape(8 * n, 128), HIGH)
    root[...] = lax.rsqrt(degree)

    def scale(b, carry):
        v[b] = (x0[:, block(b)] * root[pl.ds(b, 1), :]).astype(bf16)
        return carry

    lax.fori_loop(0, rb, scale, 0, unroll=2)

    zero = jnp.zeros((width, 128), f32)

    def apply(turn, v, came, back, meanwhile, done):
        ss = [send_sem.at[4 * turn + i] for i in range(4)]
        rs = [recv_sem.at[10 * turn + i] for i in range(10)]
        halo = send(v.at[pl.ds(0, bands)], ahead.at[turn], ss[2], rs[8], previous)

        def stage_one(k):
            t = partner(k)
            for c in range(2):
                stage[2 * t + c] = v[index[0, 2 * t + c]]
            return t

        def mirror_one(k):
            t = partner(k)
            for c in range(2):
                f = 2 * t + c
                mirror[f] = nn(v[index[1, f]], far[f]).astype(bf16)
            return t

        def send_all(make, src, dst, ssem, rsems):
            make(0)
            dst[0][0:2] = src[pl.ds(2 * me, 2)]
            for g in range(GROUPS):

                def step(k, carry, g=g):
                    t = make(k)
                    send(src.at[pl.ds(2 * t, 2)], dst[g].at[pl.ds(2 * (k - g * per), 2)], ssem, rsems[g], t)
                    return carry

                lax.fori_loop(max(1, g * per), (g + 1) * per, step, 0)

        send_all(stage_one, stage, came, ss[0], rs[0:4])
        send_all(mirror_one, mirror, back, ss[1], rs[4:8])

        near[...] = jnp.zeros_like(near)

        def near_one(b, fetch):
            vb = v[b]
            out = nt(vb, diag[b]) + nn(vb, diag[b])
            for h in range(bands):
                out = out + nt(fetch(b + h + 1), sup[b, h])
                near[:, block(b + h + 1)] += nn(vb, sup[b, h])
            near[:, block(b)] += out

        def near_step(b, carry):
            near_one(b, lambda at: v[at])
            return carry

        lax.fori_loop(0, rb - bands, near_step, 0)
        halo.wait_recv()
        for b in range(rb - bands, rb):
            near_one(b, lambda at: v[at] if at < rb else ahead[turn, at - rb])
        tail = send(near.at[:, pl.ds(owned, bands * 128)], tails.at[turn], ss[3], rs[9], following)
        meanwhile()

        def arrived(ref, g, sem):
            drain(ref[g].at[pl.ds(0, part - 2 if g == 0 else part)], sem)

        for g in range(GROUPS):
            arrived(came, g, rs[g])

            def forward(i4, total, g=g):
                for i in range(4):
                    i1 = i4 * 4 + i
                    j = g * part + i1
                    total = total * keep[0, j] + nt(came[g][index[2, j]], far[index[7, j]])
                    seg[i1] = total
                return total

            lax.fori_loop(0, part // 4, forward, zero)

            def add_forward(b, carry, g=g):
                near[:, block(b)] += seg[index[4, g * rb + b]] * keep[2, g * rb + b]
                return carry

            lax.fori_loop(0, rb, add_forward, 0)
        tail.wait_recv()
        near[:, 0 : bands * 128] += tails[turn]
        for g in range(GROUPS):
            arrived(back, g, rs[4 + g])

            def backward(i4, total, g=g):
                for i in range(4):
                    i1 = i4 * 4 + i
                    j = g * part + i1
                    total = total * keep[1, j] + back[g][index[3, j]].astype(f32)
                    seg[i1] = total
                return total

            lax.fori_loop(0, part // 4, backward, zero)

            def add_backward(b, carry, g=g):
                total = near[:, block(b)] + seg[index[5, g * rb + b]] * keep[3, g * rb + b]
                if g < GROUPS - 1:
                    near[:, block(b)] = total
                else:
                    done(b, total)
                return carry

            lax.fori_loop(0, rb, add_backward, 0)
        halo.wait_send()
        tail.wait_send()
        drain(stage.at[pl.ds(0, slots - 2)], ss[0])
        drain(mirror.at[pl.ds(0, slots - 2)], ss[1])

    def first_done(b, total):
        d = root[pl.ds(b, 1), :]
        t = total * d
        t1[:, block(b)] = t
        u[b] = (t * d).astype(bf16)

    def last_done(b, total):
        t2[:, block(b)] = total * root[pl.ds(b, 1), :]

    apply(0, v, came1, back1, lambda: None, first_done)
    saves.append(pltpu.make_async_copy(t1, t1_hbm, out_sem.at[1]))
    saves[1].start()

    early = []

    def early_gram():
        (xh, xl), (ph, pl_) = halves(x0[...]), halves(t1[...])
        c00, c11 = nt(xh, xl), nt(ph, pl_)
        early.append(nt(xh, ph) + (nt(xh, pl_) + nt(xl, ph)))
        early.append(nt(ph, ph) + (c11 + c11.T))
        early.append(nt(xh, xh) + (c00 + c00.T))

    apply(1, u, came2, back2, early_gram, last_done)
    saves.append(pltpu.make_async_copy(t2, t2_hbm, out_sem.at[2]))
    saves[2].start()

    (th, tl), (xh, xl), (ph, pl_) = halves(t2[...]), halves(x0[...]), halves(t1[...])
    c22 = nt(th, tl)
    h01, h11, h00 = early
    h02 = nt(xh, th) + (nt(xh, tl) + nt(xl, th))
    h12 = nt(ph, th) + (nt(ph, tl) + nt(pl_, th))
    h22 = nt(th, th) + (c22 + c22.T)
    lanes = functools.partial(jnp.concatenate, axis=1)
    last_sum.start(jnp.concatenate([lanes([h01, h11]), lanes([h02, h12]), lanes([h22, h00])], axis=0))
    last_sum.across()
    last_sum.gather()
    new, change = coefficients(last_sum.result() * (1.0 / points), width)
    coef[...] = jnp.zeros_like(coef)
    for i in range(3):
        coef[0:width, i * width : (i + 1) * width] = new[i]
        coef[width:, i * width : (i + 1) * width] = change[i]
    for save in saves:
        save.wait()
    deg_sent.wait_send()
    drain(cols.at[pl.ds(0, n - 1)], small_sem.at[2])
    first_sum.close()
    last_sum.close()


def whole(n, tables, panel, diag_blocks, super_blocks, far_blocks):
    rb, bs = diag_blocks.shape[:2]
    bands, slots = super_blocks.shape[1], far_blocks.shape[0]
    width, owned = panel.shape
    index, keep, spread = tables
    here = pl.BlockSpec(memory_space=pltpu.VMEM)
    away = pl.BlockSpec(memory_space=pl.ANY)
    scalar = pl.BlockSpec(memory_space=pltpu.SMEM)
    wide = jax.ShapeDtypeStruct((width, owned), f32)
    blocks = VMEM((slots, width, bs), bf16)
    return pl.pallas_call(
        functools.partial(whole_kernel, n, rb, bands, float(n * owned)),
        out_shape=(wide, wide, wide, jax.ShapeDtypeStruct((2 * width, 4 * width), f32)),
        in_specs=[scalar, scalar, here, here, away, away, away, away],
        out_specs=(away, away, away, here),
        scratch_shapes=[
            VMEM(diag_blocks.shape, bf16),
            VMEM(super_blocks.shape, bf16),
            VMEM(far_blocks.shape, bf16),
            VMEM((width, owned), f32),
            VMEM((width, owned), f32),
            VMEM((width, owned), f32),
            VMEM((rb, width, bs), bf16),
            VMEM((rb, width, bs), bf16),
            VMEM((rb, bs), f32),
            VMEM((2, bands, width, bs), bf16),
            VMEM((width, owned + bands * bs), f32),
            *[blocks] * 2,
            VMEM((slots // GROUPS, width, bs), f32),
            VMEM((2, width, bands * bs), f32),
            VMEM((rb + 8, bs), f32),
            VMEM((slots, bs), f32),
            VMEM((n, 8, bs), f32),
            VMEM((n, 8, bs), f32),
            VMEM((8, bs), f32),
            DMA((4,)),
            DMA((3,)),
            DMA((4,)),
            DMA((8,)),
            DMA((20,)),
            *[VMEM((slots // GROUPS, width, bs), bf16)] * (4 * GROUPS),
            *Reduction.scratch(width),
            *Reduction.scratch(3 * width),
        ],
        compiler_params=pltpu.CompilerParams(collective_id=1, has_side_effects=True, vmem_limit_bytes=VM_LIMIT),
        name="whole",
    )(index, keep, index, spread, panel, diag_blocks, super_blocks, far_blocks)


def combine_kernel(coef, x0, t1, t2, basis, update):
    w = x0.shape[0]
    out = nn3(coef[:, 0 : 3 * w], jnp.concatenate([x0[...], t1[...], t2[...]], axis=0))
    basis[...] = out[:w]
    update[...] = out[w:]


def combine(coef, x0, t1, t2):
    w, owned = x0.shape
    chunk = 2048
    panel = pl.BlockSpec((w, chunk), lambda i: (0, i))
    return pl.pallas_call(
        combine_kernel,
        grid=(owned // chunk,),
        out_shape=(jax.ShapeDtypeStruct((w, owned), f32),) * 2,
        in_specs=[pl.BlockSpec(coef.shape, lambda i: (0, 0)), panel, panel, panel],
        out_specs=(panel, panel),
        compiler_params=pltpu.CompilerParams(vmem_limit_bytes=VM_LIMIT),
        name="combine",
    )(coef, x0, t1, t2)


def tables_kernel(n, rb, far_row, send_slot, index, keep, spread):
    slots = far_row.shape[1]
    part = slots // GROUPS
    _, y, x, z, c = position()
    lane = lax.broadcasted_iota(i32, (1, slots), 1)
    other = lane // 2
    dz = (z - (other // 2) % 4 + 4) % 4
    group = (y - other // 32 - dz + 8) % 4
    place = (((x - (other // 8) % 4 - dz + 8) % 4) * 8 + dz * 2 + (c + other) % 2) * 2 + lane % 2
    rows, lanes = (lax.broadcasted_iota(i32, (slots, slots), d) for d in (0, 1))
    same = rows == lanes
    send, far = send_slot[...], far_row[...]
    index[...] = jnp.zeros_like(index)
    keep[...] = jnp.zeros_like(keep)
    index[0:1] = jnp.maximum(send, 0)
    index[1:2] = jnp.maximum(far, 0)
    index[6:7] = far
    places = jnp.sum(jnp.where(same, jnp.broadcast_to(place, same.shape), 0), axis=1, keepdims=True)
    stride = rb + 2
    target = (lane // rb) * stride + lane % rb + 1
    for at, key in ((0, far), (1, send)):
        kind = group * stride + key + 1
        mixed = kind * slots + lane
        column = jnp.sum(jnp.where(same, jnp.broadcast_to(mixed, same.shape), 0), axis=1, keepdims=True)
        rank = jnp.sum((mixed < column).astype(i32), axis=1, keepdims=True)
        hit = rank == lanes
        ranked = jnp.sum(jnp.where(hit, jnp.broadcast_to(column, hit.shape), 0), axis=0, keepdims=True)
        order = jnp.sum(jnp.where(hit, jnp.broadcast_to(places, hit.shape), 0), axis=0, keepdims=True)
        if at == 0:
            index[7:8] = ranked % slots
        ranked = ranked // slots
        before = jnp.concatenate([jnp.full((1, 1), -1, i32), ranked[:, :-1]], axis=1)
        kinds = column // slots
        last = jnp.sum((kinds <= target).astype(i32), axis=0, keepdims=True) - 1
        found = jnp.sum((kinds == target).astype(i32), axis=0, keepdims=True)
        index[2 + at : 3 + at] = order
        index[4 + at : 5 + at] = jnp.clip(last - (lane // rb) * part, 0, part - 1)
        keep[at : at + 1] = jnp.where(lane % part == 0, 0.0, (ranked == before).astype(f32))
        keep[2 + at : 3 + at] = (found > 0).astype(f32)
    wide = lax.broadcasted_iota(i32, (slots, 8 * n), 1)
    slot = lax.broadcasted_iota(i32, (slots, 8 * n), 0)
    pairs = ((wide // 8 == slot // 2) & (wide % 8 == slot % 2)).astype(bf16)
    some = jnp.broadcast_to((send + 1).astype(f32), (16, slots)).astype(bf16)
    spread[...] = nn(some, pairs)[0:8].astype(i32) - 1


def tables_of(n, rb, far_row, send_slot):
    slots = far_row.shape[0]
    here = pl.BlockSpec(memory_space=pltpu.VMEM)
    return pl.pallas_call(
        functools.partial(tables_kernel, n, rb),
        out_shape=(
            jax.ShapeDtypeStruct((8, slots), i32),
            jax.ShapeDtypeStruct((8, slots), f32),
            jax.ShapeDtypeStruct((8, 8 * n), i32),
        ),
        in_specs=[here, here],
        out_specs=(here, here, here),
        name="tables",
    )(far_row.reshape(1, slots), send_slot.reshape(1, slots))


def shards(diag_blocks, super_blocks, far_blocks, far_row, send_slot, panel):
    n = lax.axis_size("curve")
    tables = tables_of(n, diag_blocks.shape[0], far_row, send_slot)
    x0, t1, t2, coef = whole(n, tables, panel, diag_blocks, super_blocks, far_blocks)
    return combine(coef, x0, t1, t2)


def solution(mesh):
    return jax.shard_map(
        shards,
        mesh=mesh,
        in_specs=(
            P("curve", None, None),
            P("curve", None, None, None),
            P("curve", None, None),
            P("curve"),
            P("curve"),
            P(None, "curve"),
        ),
        out_specs=(P(None, "curve"), P(None, "curve")),
        check_vma=False,
    )
```

time: 962 us -> 304 us (0.32)
  blocking collectives: 326 us -> 0 us
  Pallas kernels: 0 us -> 303 us
  other arithmetic: 196 us -> 0 us
  matrix products: 189 us -> 0 us
  waiting for transfers between devices: 130 us -> 0 us
  starting transfers between devices: 59.2 us -> 0 us
  local copies, waits for them, and re-layouts: 50.7 us -> 0 us
    psum x5 -> x0, blocking collectives: 326 us -> none  [the longest x2 134 us: shards(): rayleigh = lax.psum(gram_of(current, image), 'curve') / total_points]
    pallas_call x0 -> x3, Pallas kernels: none -> 303 us  [the longest x1 294 us: whole(): pl.pallas_call(functools.partial(whole_kernel, n, rb, bands, float(n * ow...]
    dot_general x46 -> x0, matrix products: 188 us -> none  [the longest x12 42.3 us: near_apply(): jnp.einsum('bcp,bpq->bcq', behind, supers_ext[first:first + rows_dev, ban...]
    scatter-add x6 -> x0, other arithmetic: 135 us -> none  [the longest x3 67.6 us: apply_w(): result = result.at[send_index].add(jnp.where(send_live, returned, 0.0))]
    all_to_all x6 -> x0, waiting for transfers between devices: 130 us -> none  [the longest x3 76.9 us: apply_w(): lax.all_to_all(mirror, 'curve', split_axis=0, concat_axis=0, tiled=True)]
    all_to_all x6 -> x0, starting transfers between devices: 51.4 us -> none  [the longest x3 32.9 us: apply_w(): lax.all_to_all(outgoing, 'curve', split_axis=0, concat_axis=0, tiled=True)]
    another operation x15 -> x0, other arithmetic: 36.2 us -> none  [the longest x9 19.6 us: lower_inverse(): factor = jnp.linalg.cholesky(cross)]
    select_n x6 -> x0, other arithmetic: 21 us -> none  [the longest x2 12.1 us: apply_w(): result = result.at[send_index].add(jnp.where(send_live, returned, 0.0))]
  transfers between devices with their start and end apart: 13 -> 0, of which waited for: 4 -> 0; matrix products, arithmetic and copies ran while one was open for 28% -> 0% of each run, Pallas kernels for 0% -> 0%
where the time goes in v2:
time: 304 us; the launch traced here: 303 us
  Pallas kernels  303 us (100%)
    pallas_call x1, Pallas kernels, whole(): pl.pallas_call(functools.partial(whole_kernel, n, rb, bands, float(n * ow...  294 us
    pallas_call x1, Pallas kernels, combine(): pl.pallas_call(combine_kernel, grid=(owned // chunk,), out_shape=(jax.Sha...  6.36 us

profile of v2, /device:TPU:1, one launch (start us, length us, event | category | flops | bytes accessed | tf_op | source)
XLA Modules:
  0.0 303.4 jit_solution(9003391499107686569)
XLA Ops:
  0.6 2.2 tables.1
  2.8 294.2 %whole.1 = (f32[64,8192]{1,0:T(8,128)}, f32[64,8192]{1,0:T(8,128)}, f32[64,8192]{1,0:T(8,128)}, f32[128,256]{1,0:T(8,128)}) custom-call(s32[8,256]{1,0:T(8,128)} %get-tuple-element.9.index.index_v, f32[8,256]{1,0:T(8,128)} %get-tuple-element.10.keep, s32[8,256]{1,0:T(8,128)} %get-tuple-element.9.index.index_v, s32[8,1024]{1,0:T(8,128)} %get-tuple-element.11.spread, ...), custom_call_target="tpu_custom_call" | custom-call | tf_op jit(solution)/shard_map/whole/pallas_call | solution.py:455
  297.1 6.4 %combine.1 = (f32[64,8192]{1,0:T(8,128)}, f32[64,8192]{1,0:T(8,128)}) custom-call(f32[128,256]{1,0:T(8,128)} %get-tuple-element.12.coef, f32[64,8192]{1,0:T(8,128)} %get-tuple-element.13.x0, f32[64,8192]{1,0:T(8,128)} %get-tuple-element.14.t1, f32[64,8192]{1,0:T(8,128)} %get-tuple-element.15.t2), custom_call_target="tpu_custom_call" | custom-call | tf_op jit(solution)/shard_map/combine/pallas_call | solution.py:505

commit v3 on v2

--- a/solution.py
+++ b/solution.py
@@ -154,17 +154,19 @@
 GROUPS = 4
 
 
-def coefficients(gram, w):
-    h01, h11 = gram[0:w, 0:w], gram[0:w, w:]
-    h02, h12 = gram[w : 2 * w, 0:w], gram[w : 2 * w, w:]
-    h22, h00 = gram[2 * w :, 0:w], gram[2 * w :, w:]
-    mul = functools.partial(nn, precision=HIGH)
-    mul_t = functools.partial(nt, precision=HIGH)
-    one = eye(w)
-    y0 = one - STEP * h01.T
+mul = functools.partial(nn, precision=HIGH)
+mul_t = functools.partial(nt, precision=HIGH)
+
+
+def first_step(h00, h01, h11):
+    y0 = eye(h00.shape[0]) - STEP * h01.T
     part = mul(y0, h01)
     m1 = chol_inverse(mul_t(mul(y0, h00), y0) + STEP * (part + part.T) + STEP * STEP * h11)
-    a0, a1 = mul(m1, y0), STEP * m1
+    return mul(m1, y0), STEP * m1
+
+
+def second_step(h00, h01, h11, a0, a1, h02, h12, h22):
+    one = eye(h00.shape[0])
     s01 = mul_t(h01, a0) + mul_t(h02, a1)
     s11 = mul_t(h11, a0) + mul_t(h12, a1)
     rayleigh = mul(a0, s01) + mul(a1, s11)
@@ -182,7 +184,7 @@
 
 def whole_kernel(
     n, rb, bands, points,
-    index, keep, index_v, spread, panel_hbm, diag_hbm, super_hbm, far_hbm,
+    index, keep, index_v, panel_hbm, diag_hbm, super_hbm, far_hbm,
     x_hbm, t1_hbm, t2_hbm, coef,
     diag, sup, far, x0, t1, t2, v, u, root, ahead, near, stage, mirror, seg, tails,
     deg, far_sums, cols, cols_in, deg_tail, load_sem, out_sem, small_sem, send_sem, recv_sem, *rest,
@@ -206,11 +208,11 @@
 
     @pl.loop(1, n)
     def _(k):
-        pl.semaphore_signal(barrier, inc=1, device_id=(partner(k),), device_id_type=MESH)
+        pl.semaphore_signal(barrier, inc=1, device_id=((me + k) % n,), device_id_type=MESH)
 
     arrive, reductions = rest[: 4 * GROUPS], rest[4 * GROUPS :]
     came1, back1, came2, back2 = (arrive[i * GROUPS : (i + 1) * GROUPS] for i in range(4))
-    first_sum, last_sum = Reduction(reductions[:6]), Reduction(reductions[6:])
+    first_sum, mid_sum, last_sum = (Reduction(reductions[i : i + 6]) for i in (0, 6, 12))
     following, previous = (me + 1) % n, (me + n - 1) % n
 
     loads[0].wait()
@@ -236,37 +238,36 @@
 
     loads[1].wait()
     loads[2].wait()
-    lax.fori_loop(0, rb // 2, near_degree, 0)
+    lax.fori_loop(0, rb // 2, near_degree, 0, unroll=4)
     pl.semaphore_wait(barrier, n - 1)
     first_sum.start(jnp.concatenate([gram, jnp.zeros_like(gram)], axis=1))
-    lax.fori_loop(rb // 2, rb, near_degree, 0)
+    lax.fori_loop(rb // 2, rb, near_degree, 0, unroll=4)
     first_sum.across()
     deg_sent = send(deg.at[pl.ds(rb, 8)], deg_tail, small_sem.at[0], small_sem.at[1], following)
     loads[3].wait()
-    sub = lax.broadcasted_iota(i32, (8, 128), 0)
 
     def far_degree(k):
         t = partner(k)
-        pair = []
         for c in range(2):
             f = 2 * t + c
             far_sums[pl.ds(f, 1), :] = row_sums(far[f])
-            pair.append(column_sums(far[f]))
-        cols[t] = jnp.where(sub == 0, pair[0], jnp.where(sub == 1, pair[1], 0.0))
+            cols[f] = column_sums(far[f])
         return t
 
     def far_step(k, carry):
         t = far_degree(k)
-        send(cols.at[t], cols_in.at[me], small_sem.at[2], small_sem.at[3], t)
+        send(cols.at[pl.ds(2 * t, 2)], cols_in.at[pl.ds(2 * me, 2)], small_sem.at[2], small_sem.at[3], t)
         return carry
 
     far_degree(0)
-    cols_in[me] = cols[me]
-    lax.fori_loop(1, n // 2, far_step, 0)
+    cols_in[pl.ds(2 * me, 2)] = cols[pl.ds(2 * me, 2)]
+    lax.fori_loop(1, n // 2 + 1, far_step, 0, unroll=4)
     first_sum.gather()
-    lax.fori_loop(n // 2, n, far_step, 0)
-
-    inverse = chol_inverse(first_sum.result()[:, :width] * (1.0 / points))
+    lax.fori_loop(n // 2 + 1, n, far_step, 0, unroll=3)
+
+    gram = first_sum.result()[:, :width] * (1.0 / points)
+    inverse = chol_inverse(gram)
+    h00 = mul_t(mul(inverse, gram), inverse)
     x0[...] = nn3(inverse, panel[...])
     saves = [pltpu.make_async_copy(x0, x_hbm, out_sem.at[0])]
     saves[0].start()
@@ -275,10 +276,16 @@
     degree = deg[0:rb, :] + nn((owner_rows == index_v[6:7, :]).astype(f32), far_sums[...], HIGH)
     deg_sent.wait_recv()
     degree = degree + jnp.concatenate([deg_tail[...], jnp.zeros((rb - 8, 128), f32)], axis=0)
-    slot_rows = lax.broadcasted_iota(i32, (rb, 8 * n), 0)
-    chosen = (slot_rows == spread[0:1, :]).astype(f32)
-    drain(cols_in.at[pl.ds(0, n - 1)], small_sem.at[3])
-    degree = degree + nn(chosen, cols_in[...].reshape(8 * n, 128), HIGH)
+    slot_rows = lax.broadcasted_iota(i32, (rb, slots), 0)
+    chosen = (slot_rows == index_v[8:9, :]).astype(f32)
+    drain(cols_in.at[pl.ds(0, slots - 2)], small_sem.at[3])
+
+    def unpack(f, carry):
+        far_sums[pl.ds(f, 1), :] = cols_in[f]
+        return carry
+
+    lax.fori_loop(0, slots, unpack, 0, unroll=8)
+    degree = degree + nn(chosen, far_sums[...], HIGH)
     root[...] = lax.rsqrt(degree)
 
     def scale(b, carry):
@@ -289,7 +296,7 @@
 
     zero = jnp.zeros((width, 128), f32)
 
-    def apply(turn, v, came, back, meanwhile, done):
+    def apply(turn, v, came, back, hooks, done):
         ss = [send_sem.at[4 * turn + i] for i in range(4)]
         rs = [recv_sem.at[10 * turn + i] for i in range(10)]
         halo = send(v.at[pl.ds(0, bands)], ahead.at[turn], ss[2], rs[8], previous)
@@ -307,10 +314,11 @@
                 mirror[f] = nn(v[index[1, f]], far[f]).astype(bf16)
             return t
 
-        def send_all(make, src, dst, ssem, rsems):
-            make(0)
-            dst[0][0:2] = src[pl.ds(2 * me, 2)]
-            for g in range(GROUPS):
+        def send_groups(make, src, dst, ssem, rsems, groups):
+            if 0 in groups:
+                make(0)
+                dst[0][0:2] = src[pl.ds(2 * me, 2)]
+            for g in groups:
 
                 def step(k, carry, g=g):
                     t = make(k)
@@ -319,8 +327,10 @@
 
                 lax.fori_loop(max(1, g * per), (g + 1) * per, step, 0)
 
-        send_all(stage_one, stage, came, ss[0], rs[0:4])
-        send_all(mirror_one, mirror, back, ss[1], rs[4:8])
+        hooks[0]()
+        send_groups(stage_one, stage, came, ss[0], rs[0:4], range(GROUPS))
+        hooks[1]()
+        send_groups(mirror_one, mirror, back, ss[1], rs[4:8], range(GROUPS // 2))
 
         near[...] = jnp.zeros_like(near)
 
@@ -341,7 +351,8 @@
         for b in range(rb - bands, rb):
             near_one(b, lambda at: v[at] if at < rb else ahead[turn, at - rb])
         tail = send(near.at[:, pl.ds(owned, bands * 128)], tails.at[turn], ss[3], rs[9], following)
-        meanwhile()
+        hooks[2]()
+        send_groups(mirror_one, mirror, back, ss[1], rs[4:8], range(GROUPS // 2, GROUPS))
 
         def arrived(ref, g, sem):
             drain(ref[g].at[pl.ds(0, part - 2 if g == 0 else part)], sem)
@@ -366,6 +377,7 @@
             lax.fori_loop(0, rb, add_forward, 0)
         tail.wait_recv()
         near[:, 0 : bands * 128] += tails[turn]
+        hooks[3]()
         for g in range(GROUPS):
             arrived(back, g, rs[4 + g])
 
@@ -387,7 +399,7 @@
                     done(b, total)
                 return carry
 
-            lax.fori_loop(0, rb, add_backward, 0)
+            lax.fori_loop(0, rb, add_backward, 0, unroll=4)
         halo.wait_send()
         tail.wait_send()
         drain(stage.at[pl.ds(0, slots - 2)], ss[0])
@@ -402,34 +414,38 @@
     def last_done(b, total):
         t2[:, block(b)] = total * root[pl.ds(b, 1), :]
 
-    apply(0, v, came1, back1, lambda: None, first_done)
+    apply(0, v, came1, back1, [lambda: None] * 4, first_done)
     saves.append(pltpu.make_async_copy(t1, t1_hbm, out_sem.at[1]))
     saves[1].start()
 
-    early = []
+    kept = []
+    lanes = functools.partial(jnp.concatenate, axis=1)
 
     def early_gram():
         (xh, xl), (ph, pl_) = halves(x0[...]), halves(t1[...])
-        c00, c11 = nt(xh, xl), nt(ph, pl_)
-        early.append(nt(xh, ph) + (nt(xh, pl_) + nt(xl, ph)))
-        early.append(nt(ph, ph) + (c11 + c11.T))
-        early.append(nt(xh, xh) + (c00 + c00.T))
-
-    apply(1, u, came2, back2, early_gram, last_done)
+        c11 = nt(ph, pl_)
+        h01 = nt(xh, ph) + (nt(xh, pl_) + nt(xl, ph))
+        mid_sum.start(lanes([h01, nt(ph, ph) + (c11 + c11.T)]))
+
+    def early_step():
+        sums = mid_sum.result() * (1.0 / points)
+        h01, h11 = sums[:, :width], sums[:, width:]
+        kept.extend((h00, h01, h11, *first_step(h00, h01, h11)))
+
+    apply(1, u, came2, back2, [early_gram, mid_sum.across, mid_sum.gather, early_step], last_done)
     saves.append(pltpu.make_async_copy(t2, t2_hbm, out_sem.at[2]))
     saves[2].start()
 
     (th, tl), (xh, xl), (ph, pl_) = halves(t2[...]), halves(x0[...]), halves(t1[...])
     c22 = nt(th, tl)
-    h01, h11, h00 = early
     h02 = nt(xh, th) + (nt(xh, tl) + nt(xl, th))
     h12 = nt(ph, th) + (nt(ph, tl) + nt(pl_, th))
     h22 = nt(th, th) + (c22 + c22.T)
-    lanes = functools.partial(jnp.concatenate, axis=1)
-    last_sum.start(jnp.concatenate([lanes([h01, h11]), lanes([h02, h12]), lanes([h22, h00])], axis=0))
+    last_sum.start(jnp.concatenate([lanes([h02, h12]), lanes([h22, jnp.zeros_like(h22)])], axis=0))
     last_sum.across()
     last_sum.gather()
-    new, change = coefficients(last_sum.result() * (1.0 / points), width)
+    sums = last_sum.result() * (1.0 / points)
+    new, change = second_step(*kept, sums[:width, :width], sums[:width, width:], sums[width:, :width])
     coef[...] = jnp.zeros_like(coef)
     for i in range(3):
         coef[0:width, i * width : (i + 1) * width] = new[i]
@@ -437,8 +453,9 @@
     for save in saves:
         save.wait()
     deg_sent.wait_send()
-    drain(cols.at[pl.ds(0, n - 1)], small_sem.at[2])
+    drain(cols.at[pl.ds(0, slots - 2)], small_sem.at[2])
     first_sum.close()
+    mid_sum.close()
     last_sum.close()
 
 
@@ -446,7 +463,7 @@
     rb, bs = diag_blocks.shape[:2]
     bands, slots = super_blocks.shape[1], far_blocks.shape[0]
     width, owned = panel.shape
-    index, keep, spread = tables
+    index, keep = tables
     here = pl.BlockSpec(memory_space=pltpu.VMEM)
     away = pl.BlockSpec(memory_space=pl.ANY)
     scalar = pl.BlockSpec(memory_space=pltpu.SMEM)
@@ -455,7 +472,7 @@
     return pl.pallas_call(
         functools.partial(whole_kernel, n, rb, bands, float(n * owned)),
         out_shape=(wide, wide, wide, jax.ShapeDtypeStruct((2 * width, 4 * width), f32)),
-        in_specs=[scalar, scalar, here, here, away, away, away, away],
+        in_specs=[scalar, scalar, here, away, away, away, away],
         out_specs=(away, away, away, here),
         scratch_shapes=[
             VMEM(diag_blocks.shape, bf16),
@@ -474,8 +491,8 @@
             VMEM((2, width, bands * bs), f32),
             VMEM((rb + 8, bs), f32),
             VMEM((slots, bs), f32),
-            VMEM((n, 8, bs), f32),
-            VMEM((n, 8, bs), f32),
+            VMEM((slots, 1, bs), f32),
+            VMEM((slots, 1, bs), f32),
             VMEM((8, bs), f32),
             DMA((4,)),
             DMA((3,)),
@@ -484,11 +501,12 @@
             DMA((20,)),
             *[VMEM((slots // GROUPS, width, bs), bf16)] * (4 * GROUPS),
             *Reduction.scratch(width),
-            *Reduction.scratch(3 * width),
+            *Reduction.scratch(width),
+            *Reduction.scratch(2 * width),
         ],
         compiler_params=pltpu.CompilerParams(collective_id=1, has_side_effects=True, vmem_limit_bytes=VM_LIMIT),
         name="whole",
-    )(index, keep, index, spread, panel, diag_blocks, super_blocks, far_blocks)
+    )(index, keep, index, panel, diag_blocks, super_blocks, far_blocks)
 
 
 def combine_kernel(coef, x0, t1, t2, basis, update):
@@ -500,7 +518,7 @@
 
 def combine(coef, x0, t1, t2):
     w, owned = x0.shape
-    chunk = 2048
+    chunk = 1024
     panel = pl.BlockSpec((w, chunk), lambda i: (0, i))
     return pl.pallas_call(
         combine_kernel,
@@ -513,7 +531,7 @@
     )(coef, x0, t1, t2)
 
 
-def tables_kernel(n, rb, far_row, send_slot, index, keep, spread):
+def tables_kernel(n, rb, far_row, send_slot, index, keep):
     slots = far_row.shape[1]
     part = slots // GROUPS
     _, y, x, z, c = position()
@@ -530,6 +548,7 @@
     index[0:1] = jnp.maximum(send, 0)
     index[1:2] = jnp.maximum(far, 0)
     index[6:7] = far
+    index[8:9] = send
     places = jnp.sum(jnp.where(same, jnp.broadcast_to(place, same.shape), 0), axis=1, keepdims=True)
     stride = rb + 2
     target = (lane // rb) * stride + lane % rb + 1
@@ -552,11 +571,6 @@
         index[4 + at : 5 + at] = jnp.clip(last - (lane // rb) * part, 0, part - 1)
         keep[at : at + 1] = jnp.where(lane % part == 0, 0.0, (ranked == before).astype(f32))
         keep[2 + at : 3 + at] = (found > 0).astype(f32)
-    wide = lax.broadcasted_iota(i32, (slots, 8 * n), 1)
-    slot = lax.broadcasted_iota(i32, (slots, 8 * n), 0)
-    pairs = ((wide // 8 == slot // 2) & (wide % 8 == slot % 2)).astype(bf16)
-    some = jnp.broadcast_to((send + 1).astype(f32), (16, slots)).astype(bf16)
-    spread[...] = nn(some, pairs)[0:8].astype(i32) - 1
 
 
 def tables_of(n, rb, far_row, send_slot):
@@ -565,12 +579,11 @@
     return pl.pallas_call(
         functools.partial(tables_kernel, n, rb),
         out_shape=(
-            jax.ShapeDtypeStruct((8, slots), i32),
+            jax.ShapeDtypeStruct((16, slots), i32),
             jax.ShapeDtypeStruct((8, slots), f32),
-            jax.ShapeDtypeStruct((8, 8 * n), i32),
         ),
         in_specs=[here, here],
-        out_specs=(here, here, here),
+        out_specs=(here, here),
         name="tables",
     )(far_row.reshape(1, slots), send_slot.reshape(1, slots))
 

time: 304 us -> 293 us (0.964)
  Pallas kernels: 303 us -> 292 us
    pallas_call x1, Pallas kernels: 294 us -> 282 us  [whole(): pl.pallas_call(functools.partial(whole_kernel, n, rb, bands, float(n * ow...]
where the time goes in v3:
time: 293 us
  Pallas kernels  292 us (100%)
    pallas_call x1, Pallas kernels, whole(): pl.pallas_call(functools.partial(whole_kernel, n, rb, bands, float(n * ow...  282 us
    pallas_call x1, Pallas kernels, combine(): pl.pallas_call(combine_kernel, grid=(owned // chunk,), out_shape=(jax.Sha...  8.14 us

profile of v3, /device:TPU:1, one launch (start us, length us, event | category | flops | bytes accessed | tf_op | source)
XLA Modules:
  0.0 292.7 jit_solution(6631774600105300493)
XLA Ops:
  0.6 2.1 tables.1
  2.8 281.8 %whole.1 = (f32[64,8192]{1,0:T(8,128)}, f32[64,8192]{1,0:T(8,128)}, f32[64,8192]{1,0:T(8,128)}, f32[128,256]{1,0:T(8,128)}) custom-call(s32[16,256]{1,0:T(8,128)} %get-tuple-element.8.index.index_v, f32[8,256]{1,0:T(8,128)} %get-tuple-element.9.keep, s32[16,256]{1,0:T(8,128)} %get-tuple-element.8.index.index_v, f32[64,8192]{1,0:T(8,128)} %panel_hbm.1, ...), custom_call_target="tpu_custom_call" | custom-call | tf_op jit(solution)/shard_map/whole/pallas_call | solution.py:472
  284.6 8.1 %combine.1 = (f32[64,8192]{1,0:T(8,128)}, f32[64,8192]{1,0:T(8,128)}) custom-call(f32[128,256]{1,0:T(8,128)} %get-tuple-element.10.coef, f32[64,8192]{1,0:T(8,128)} %get-tuple-element.11.x0, f32[64,8192]{1,0:T(8,128)} %get-tuple-element.12.t1, f32[64,8192]{1,0:T(8,128)} %get-tuple-element.13.t2), custom_call_target="tpu_custom_call" | custom-call | tf_op jit(solution)/shard_map/combine/pallas_call | solution.py:523

commit v4 on v3

--- a/solution.py
+++ b/solution.py
@@ -48,21 +48,35 @@
 
 def chol_inverse(cross):
     n = cross.shape[0]
-    both = jnp.concatenate([cross, eye(n)], axis=1)
+    rows, lanes = (lax.broadcasted_iota(i32, (n, n), d) for d in (0, 1))
+    diagonal = jnp.where(rows == lanes, cross, 0.0)
+    down = lax.rsqrt(jnp.sum(diagonal, axis=1, keepdims=True))
+    along = lax.rsqrt(jnp.sum(diagonal, axis=0, keepdims=True))
+    both = jnp.concatenate([cross * down * along, eye(n)], axis=1)
     tiles = [both[8 * i : 8 * i + 8] for i in range(n // 8)]
     row_id = lax.broadcasted_iota(i32, (8, 1), 0)
-    for k in range(n):
+    for k in range(0, n, 2):
         at, sub = k // 8, k % 8
-        row = tiles[at][sub : sub + 1]
-        row = row / row[:, k : k + 1]
+        r0, r1 = tiles[at][sub : sub + 1], tiles[at][sub + 1 : sub + 2]
+        a, b, d = r0[:, k : k + 1], r0[:, k + 1 : k + 2], r1[:, k + 1 : k + 2]
+        scale = 1.0 / (a * d - b * b)
+        p0, p1 = (d * r0 - b * r1) * scale, (a * r1 - b * r0) * scale
         for i in range(at, n // 8):
-            column = tiles[i][:, k : k + 1]
+            if i == at and sub == 6:
+                continue
+            c0, c1 = tiles[i][:, k : k + 1], tiles[i][:, k + 1 : k + 2]
             if i == at:
-                column = jnp.where(row_id > sub, column, 0.0)
-            tiles[i] = tiles[i] - column * row
+                c0, c1 = (jnp.where(row_id > sub + 1, c, 0.0) for c in (c0, c1))
+            tiles[i] = tiles[i] - (c0 * p0 + c1 * p1)
     both = jnp.concatenate(tiles, axis=0)
-    pivots = jnp.sum(both[:, :n] * eye(n), axis=1, keepdims=True)
-    return both[:, n:] * lax.rsqrt(pivots)
+    left, right = both[:, :n], both[:, n:]
+    odd = lax.broadcasted_iota(i32, (n, 1), 0) % 2 == 1
+    own = jnp.sum(jnp.where(rows == lanes, left, 0.0), axis=1, keepdims=True)
+    side = jnp.sum(jnp.where(rows == lanes + 1, left, 0.0), axis=1, keepdims=True)
+    above = jnp.concatenate([own[:1], own[:-1]], axis=0)
+    ratio = jnp.where(odd, side / above, 0.0)
+    upper = jnp.concatenate([right[:1], right[:-1]], axis=0)
+    return (right - ratio * upper) * lax.rsqrt(own - ratio * side) * along
 
 
 def position():
@@ -222,48 +236,59 @@
     deg[...] = jnp.zeros_like(deg)
     ones = jnp.ones((16, 128), bf16)
 
-    def row_sums(blk):
-        return nt(ones, blk)[0:1]
-
     def column_sums(blk):
-        return jnp.sum(blk.astype(f32), axis=0, keepdims=True)
-
-    def near_degree(b, carry):
-        rows = row_sums(diag[b]) + column_sums(diag[b])
-        for h in range(bands):
-            rows = rows + row_sums(sup[b, h])
-            deg[pl.ds(b + h + 1, 1), :] += column_sums(sup[b, h])
-        deg[pl.ds(b, 1), :] += rows
+        return jnp.sum(blk, axis=0, keepdims=True)
+
+    def near_degree(b4, carry):
+        totals = []
+        for i in range(4):
+            b = b4 * 4 + i
+            total = diag[b].astype(f32)
+            deg[pl.ds(b, 1), :] += column_sums(total)
+            for h in range(bands):
+                blk = sup[b, h].astype(f32)
+                deg[pl.ds(b + h + 1, 1), :] += column_sums(blk)
+                total = total + blk
+            totals.append(total)
+        high, low = halves(jnp.concatenate(totals, axis=0))
+        rows = (nt(ones, high) + nt(ones, low))[0:1]
+        for i in range(4):
+            deg[pl.ds(b4 * 4 + i, 1), :] += rows[:, i * 128 : i * 128 + 128]
         return carry
 
     loads[1].wait()
     loads[2].wait()
-    lax.fori_loop(0, rb // 2, near_degree, 0, unroll=4)
+    lax.fori_loop(0, rb // 4, near_degree, 0)
     pl.semaphore_wait(barrier, n - 1)
     first_sum.start(jnp.concatenate([gram, jnp.zeros_like(gram)], axis=1))
-    lax.fori_loop(rb // 2, rb, near_degree, 0, unroll=4)
-    first_sum.across()
     deg_sent = send(deg.at[pl.ds(rb, 8)], deg_tail, small_sem.at[0], small_sem.at[1], following)
     loads[3].wait()
 
-    def far_degree(k):
-        t = partner(k)
-        for c in range(2):
-            f = 2 * t + c
-            far_sums[pl.ds(f, 1), :] = row_sums(far[f])
-            cols[f] = column_sums(far[f])
-        return t
-
-    def far_step(k, carry):
-        t = far_degree(k)
-        send(cols.at[pl.ds(2 * t, 2)], cols_in.at[pl.ds(2 * me, 2)], small_sem.at[2], small_sem.at[3], t)
+    def far_pair(k2, sent=(0, 1)):
+        to = [partner(2 * k2), partner(2 * k2 + 1)]
+        at = [2 * t + c for t in to for c in range(2)]
+        blocks = [far[f] for f in at]
+        rows = nt(ones, jnp.concatenate(blocks, axis=0))[0:1]
+        for i, f in enumerate(at):
+            far_sums[pl.ds(f, 1), :] = rows[:, i * 128 : i * 128 + 128]
+            cols[f] = column_sums(blocks[i].astype(f32))
+        for i in sent:
+            send(
+                cols.at[pl.ds(2 * to[i], 2)], cols_in.at[pl.ds(2 * me, 2)], small_sem.at[2], small_sem.at[3], to[i]
+            )
+
+    def far_step(k2, carry):
+        far_pair(k2)
         return carry
 
-    far_degree(0)
+    far_pair(0, (1,))
     cols_in[pl.ds(2 * me, 2)] = cols[pl.ds(2 * me, 2)]
-    lax.fori_loop(1, n // 2 + 1, far_step, 0, unroll=4)
+    third = n // 6
+    lax.fori_loop(1, third + 1, far_step, 0, unroll=3)
+    first_sum.across()
+    lax.fori_loop(third + 1, 2 * third + 1, far_step, 0, unroll=3)
     first_sum.gather()
-    lax.fori_loop(n // 2 + 1, n, far_step, 0, unroll=3)
+    lax.fori_loop(2 * third + 1, n // 2, far_step, 0, unroll=3)
 
     gram = first_sum.result()[:, :width] * (1.0 / points)
     inverse = chol_inverse(gram)
@@ -518,7 +543,7 @@
 
 def combine(coef, x0, t1, t2):
     w, owned = x0.shape
-    chunk = 1024
+    chunk = 4096
     panel = pl.BlockSpec((w, chunk), lambda i: (0, i))
     return pl.pallas_call(
         combine_kernel,

time: 293 us -> 278 us (0.949)
  Pallas kernels: 292 us -> 278 us
    pallas_call x1, Pallas kernels: 282 us -> 270 us  [whole(): pl.pallas_call(functools.partial(whole_kernel, n, rb, bands, float(n * ow...]
where the time goes in v4:
time: 278 us
  Pallas kernels  278 us (100%)
    pallas_call x1, Pallas kernels, whole(): pl.pallas_call(functools.partial(whole_kernel, n, rb, bands, float(n * ow...  270 us
    pallas_call x1, Pallas kernels, combine(): pl.pallas_call(combine_kernel, grid=(owned // chunk,), out_shape=(jax.Sha...  5.77 us

profile of v4, /device:TPU:1, one launch (start us, length us, event | category | flops | bytes accessed | tf_op | source)
XLA Modules:
  0.0 278.3 jit_solution(2106773215077670852)
XLA Ops:
  0.6 2.1 tables.1
  2.8 269.7 %whole.1 = (f32[64,8192]{1,0:T(8,128)}, f32[64,8192]{1,0:T(8,128)}, f32[64,8192]{1,0:T(8,128)}, f32[128,256]{1,0:T(8,128)}) custom-call(s32[16,256]{1,0:T(8,128)} %get-tuple-element.8.index.index_v, f32[8,256]{1,0:T(8,128)} %get-tuple-element.9.keep, s32[16,256]{1,0:T(8,128)} %get-tuple-element.8.index.index_v, f32[64,8192]{1,0:T(8,128)} %panel_hbm.1, ...), custom_call_target="tpu_custom_call" | custom-call | tf_op jit(solution)/shard_map/whole/pallas_call | solution.py:497
  272.5 5.8 %combine.1 = (f32[64,8192]{1,0:T(8,128)}, f32[64,8192]{1,0:T(8,128)}) custom-call(f32[128,256]{1,0:T(8,128)} %get-tuple-element.10.coef, f32[64,8192]{1,0:T(8,128)} %get-tuple-element.11.x0, f32[64,8192]{1,0:T(8,128)} %get-tuple-element.12.t1, f32[64,8192]{1,0:T(8,128)} %get-tuple-element.13.t2), custom_call_target="tpu_custom_call" | custom-call | tf_op jit(solution)/shard_map/combine/pallas_call | solution.py:548

commit v5 on v4

--- a/solution.py
+++ b/solution.py
@@ -32,12 +32,7 @@
 
 def nn3(a, b):
     (ah, al), (bh, bl) = halves(a), halves(b)
-    return nn(ah, bh) + (nn(ah, bl) + nn(al, bh))
-
-
-def nt3(a, b):
-    (ah, al), (bh, bl) = halves(a), halves(b)
-    return nt(ah, bh) + (nt(ah, bl) + nt(al, bh))
+    return nn(jnp.concatenate([ah, ah, al], axis=1), jnp.concatenate([bh, bl, bh], axis=0))
 
 
 def eye(n, m=None):
@@ -220,8 +215,9 @@
         load.start()
     barrier = pltpu.get_barrier_semaphore()
 
-    @pl.loop(1, n)
-    def _(k):
+    greetings = 4 * n // rb
+
+    def greet(k):
         pl.semaphore_signal(barrier, inc=1, device_id=((me + k) % n,), device_id_type=MESH)
 
     arrive, reductions = rest[: 4 * GROUPS], rest[4 * GROUPS :]
@@ -240,6 +236,13 @@
         return jnp.sum(blk, axis=0, keepdims=True)
 
     def near_degree(b4, carry):
+        for i in range(1, greetings):
+            greet(b4 * greetings + i)
+
+        @pl.when(b4 > 0)
+        def _():
+            greet(b4 * greetings)
+
         totals = []
         for i in range(4):
             b = b4 * 4 + i
@@ -462,10 +465,13 @@
     saves[2].start()
 
     (th, tl), (xh, xl), (ph, pl_) = halves(t2[...]), halves(x0[...]), halves(t1[...])
-    c22 = nt(th, tl)
-    h02 = nt(xh, th) + (nt(xh, tl) + nt(xl, th))
-    h12 = nt(ph, th) + (nt(ph, tl) + nt(pl_, th))
-    h22 = nt(th, th) + (c22 + c22.T)
+    by_high = nt(jnp.concatenate([xh, ph, th], axis=0), th)
+    low_by_high = nt(jnp.concatenate([xl, pl_, tl], axis=0), th)
+    by_low = nt(jnp.concatenate([xh, ph], axis=0), tl)
+    c22 = low_by_high[2 * width :]
+    both = by_high[: 2 * width] + (by_low + low_by_high[: 2 * width])
+    h02, h12 = both[:width], both[width:]
+    h22 = by_high[2 * width :] + (c22 + c22.T)
     last_sum.start(jnp.concatenate([lanes([h02, h12]), lanes([h22, jnp.zeros_like(h22)])], axis=0))
     last_sum.across()
     last_sum.gather()

time: 278 us -> 286 us (1.029)
  Pallas kernels: 278 us -> 285 us
    pallas_call x1, Pallas kernels: 270 us -> 277 us  [whole(): pl.pallas_call(functools.partial(whole_kernel, n, rb, bands, float(n * ow...]
where the time goes in v5:
time: 286 us
  Pallas kernels  285 us (100%)
    pallas_call x1, Pallas kernels, whole(): pl.pallas_call(functools.partial(whole_kernel, n, rb, bands, float(n * ow...  277 us
    pallas_call x1, Pallas kernels, combine(): pl.pallas_call(combine_kernel, grid=(owned // chunk,), out_shape=(jax.Sha...  5.91 us

profile of v5, /device:TPU:1, one launch (start us, length us, event | category | flops | bytes accessed | tf_op | source)
XLA Modules:
  0.0 286.1 jit_solution(2932242989473110662)
XLA Ops:
  0.6 2.1 tables.1
  2.8 277.4 %whole.1 = (f32[64,8192]{1,0:T(8,128)}, f32[64,8192]{1,0:T(8,128)}, f32[64,8192]{1,0:T(8,128)}, f32[128,256]{1,0:T(8,128)}) custom-call(s32[16,256]{1,0:T(8,128)} %get-tuple-element.8.index.index_v, f32[8,256]{1,0:T(8,128)} %get-tuple-element.9.keep, s32[16,256]{1,0:T(8,128)} %get-tuple-element.8.index.index_v, f32[64,8192]{1,0:T(8,128)} %panel_hbm.1, ...), custom_call_target="tpu_custom_call" | custom-call | tf_op jit(solution)/shard_map/whole/pallas_call | solution.py:503
  280.2 5.9 %combine.1 = (f32[64,8192]{1,0:T(8,128)}, f32[64,8192]{1,0:T(8,128)}) custom-call(f32[128,256]{1,0:T(8,128)} %get-tuple-element.10.coef, f32[64,8192]{1,0:T(8,128)} %get-tuple-element.11.x0, f32[64,8192]{1,0:T(8,128)} %get-tuple-element.12.t1, f32[64,8192]{1,0:T(8,128)} %get-tuple-element.13.t2), custom_call_target="tpu_custom_call" | custom-call | tf_op jit(solution)/shard_map/combine/pallas_call | solution.py:554

commit v6 on v4

--- a/solution.py
+++ b/solution.py
@@ -462,10 +462,13 @@
     saves[2].start()
 
     (th, tl), (xh, xl), (ph, pl_) = halves(t2[...]), halves(x0[...]), halves(t1[...])
-    c22 = nt(th, tl)
-    h02 = nt(xh, th) + (nt(xh, tl) + nt(xl, th))
-    h12 = nt(ph, th) + (nt(ph, tl) + nt(pl_, th))
-    h22 = nt(th, th) + (c22 + c22.T)
+    by_high = nt(jnp.concatenate([xh, ph, th], axis=0), th)
+    low_by_high = nt(jnp.concatenate([xl, pl_, tl], axis=0), th)
+    by_low = nt(jnp.concatenate([xh, ph], axis=0), tl)
+    c22 = low_by_high[2 * width :]
+    both = by_high[: 2 * width] + (by_low + low_by_high[: 2 * width])
+    h02, h12 = both[:width], both[width:]
+    h22 = by_high[2 * width :] + (c22 + c22.T)
     last_sum.start(jnp.concatenate([lanes([h02, h12]), lanes([h22, jnp.zeros_like(h22)])], axis=0))
     last_sum.across()
     last_sum.gather()

time: 278 us -> 281 us (1.011)
  Pallas kernels: 278 us -> 281 us
    pallas_call x1, Pallas kernels: 270 us -> 273 us  [whole(): pl.pallas_call(functools.partial(whole_kernel, n, rb, bands, float(n * ow...]
where the time goes in v6:
time: 281 us
  Pallas kernels  281 us (100%)
    pallas_call x1, Pallas kernels, whole(): pl.pallas_call(functools.partial(whole_kernel, n, rb, bands, float(n * ow...  273 us
    pallas_call x1, Pallas kernels, combine(): pl.pallas_call(combine_kernel, grid=(owned // chunk,), out_shape=(jax.Sha...  5.78 us

profile of v6, /device:TPU:1, one launch (start us, length us, event | category | flops | bytes accessed | tf_op | source)
XLA Modules:
  0.0 281.2 jit_solution(100571577463137709)
XLA Ops:
  0.6 2.1 tables.1
  2.8 272.6 %whole.1 = (f32[64,8192]{1,0:T(8,128)}, f32[64,8192]{1,0:T(8,128)}, f32[64,8192]{1,0:T(8,128)}, f32[128,256]{1,0:T(8,128)}) custom-call(s32[16,256]{1,0:T(8,128)} %get-tuple-element.8.index.index_v, f32[8,256]{1,0:T(8,128)} %get-tuple-element.9.keep, s32[16,256]{1,0:T(8,128)} %get-tuple-element.8.index.index_v, f32[64,8192]{1,0:T(8,128)} %panel_hbm.1, ...), custom_call_target="tpu_custom_call" | custom-call | tf_op jit(solution)/shard_map/whole/pallas_call | solution.py:500
  275.4 5.8 %combine.1 = (f32[64,8192]{1,0:T(8,128)}, f32[64,8192]{1,0:T(8,128)}) custom-call(f32[128,256]{1,0:T(8,128)} %get-tuple-element.10.coef, f32[64,8192]{1,0:T(8,128)} %get-tuple-element.11.x0, f32[64,8192]{1,0:T(8,128)} %get-tuple-element.12.t1, f32[64,8192]{1,0:T(8,128)} %get-tuple-element.13.t2), custom_call_target="tpu_custom_call" | custom-call | tf_op jit(solution)/shard_map/combine/pallas_call | solution.py:551
